TPU v7x, 512 devices: a whole 4x8x8 slice. The times are simulated.
512 devices in a mesh: gx: 8 (over z), gy: 8 (over y), gz: 8 (over x, core).
Axes of the slice: x: 4, y: 8, z: 8, core: 2. Of those that a mesh axis runs over, the one named last changes fastest.
Arguments:
- basis: bfloat16 [32, 128, 64, 1024], P(None, 'gx', 'gy', 'gz'), may hold values from -12 to 12
- krylov: float32 [16, 128, 64, 1024], P(None, 'gx', 'gy', 'gz'), may hold values from -12 to 12
- center: bfloat16 [128, 64, 1024], P('gx', 'gy', 'gz'), may hold values from 8 to 24
- couplings: bfloat16 [26, 128, 64, 1024], P(None, 'gx', 'gy', 'gz'), may hold values from -1 to 0.3984375
Outputs:
- projected: float32 [16, 128, 64, 1024], P(None, 'gx', 'gy', 'gz')
- coefficients: float32 [32, 16], replicated
All inputs are finite; a program needn't handle non-finite values.
Results may differ from a plain program's by a relative error of at most 0.0003.
Values sent between devices are 32-bit elements; how exact they have to be, the bound alone decides.
No kernel may reach another device: no remote copies, remote signals or barrier semaphores. Data moves between devices by JAX's collectives and lax.ppermute only.
A program may use at most 64 MiB of HBM per device.

v0:
```python
import jax
import jax.numpy as jnp
from jax import lax
from jax.sharding import PartitionSpec as P


def extended(block, sides, width):
    for axis, dim in sides:
        count = lax.axis_size(axis)
        forward = [(i, i + 1) for i in range(count - 1)]
        backward = [(target, source) for source, target in forward]
        low = lax.ppermute(
            lax.slice_in_dim(block, block.shape[dim] - width, None, axis=dim), axis, forward
        )
        high = lax.ppermute(lax.slice_in_dim(block, 0, width, axis=dim), axis, backward)
        block = jnp.concatenate([low, block, high], axis=dim)
    return block


def local(basis, krylov, center, couplings):
    count_v, size_x, size_y, size_z = krylov.shape
    count_u = basis.shape[0]
    padded = extended(krylov, (("gx", 1), ("gy", 2), ("gz", 3)), 1)
    image = center.astype(jnp.float32)[None] * krylov
    which = 0
    for step_a in (-1, 0, 1):
        for step_b in (-1, 0, 1):
            for step_c in (-1, 0, 1):
                if step_a == 0 and step_b == 0 and (step_c == 0):
                    continue
                moved = padded[
                    :,
                    1 + step_a : 1 + step_a + size_x,
                    1 + step_b : 1 + step_b + size_y,
                    1 + step_c : 1 + step_c + size_z,
                ]
                image = image + couplings[which].astype(jnp.float32)[None] * moved
                which = which + 1
    total_cells = (
        size_x * size_y * size_z * lax.axis_size("gx") * lax.axis_size("gy") * lax.axis_size("gz")
    )
    scale = 1.0 / total_cells
    flat_basis = basis.reshape(count_u, -1)
    flat_image = image.reshape(count_v, -1)
    dims = (((1,), (1,)), ((), ()))
    local_first = scale * lax.dot_general(
        flat_basis,
        flat_image,
        dims,
        precision=lax.Precision.HIGHEST,
        preferred_element_type=jnp.float32,
    )
    first = lax.psum(local_first, ("gx", "gy", "gz"))
    once = flat_image - jnp.dot(
        first.T, flat_basis, precision=lax.Precision.HIGHEST, preferred_element_type=jnp.float32
    )
    local_second = scale * lax.dot_general(
        flat_basis, once, dims, precision=lax.Precision.HIGHEST, preferred_element_type=jnp.float32
    )
    second = lax.psum(local_second, ("gx", "gy", "gz"))
    projected = once - jnp.dot(
        second.T, flat_basis, precision=lax.Precision.HIGHEST, preferred_element_type=jnp.float32
    )
    return (projected.reshape(count_v, size_x, size_y, size_z), first + second)


def solution(mesh):
    in_specs = (
        P(None, "gx", "gy", "gz"),
        P(None, "gx", "gy", "gz"),
        P("gx", "gy", "gz"),
        P(None, "gx", "gy", "gz"),
    )
    out_specs = (P(None, "gx", "gy", "gz"), P())
    return jax.shard_map(local, mesh=mesh, in_specs=in_specs, out_specs=out_specs, check_vma=False)
```

profile of v0, /device:TPU:2, one launch (start us, length us, event | category | flops | bytes accessed | tf_op | source)
XLA Modules:
  0.0 261.5 jit_solution(8697835454389444299)
XLA Ops:
  0.6 0.0 copy-start.2
  0.6 1.9 copy.8
  2.6 0.0 copy-start.1
  2.6 4.3 %collective-permute-start = (f32[16,1,8,128]{3,0,2,1:T(8,128)S(1)}, f32[16,1,8,128]{3,0,2,1:T(8,128)S(1)}, u32[]{:S(2)}, u32[]{:S(2)}) collective-permute-start(f32[16,1,8,128]{3,0,2,1:T(8,128)S(1)} %get-tuple-element.9), channel_id=1, source_target_pairs={{0,64},{64,128},{128,192},{192,256},{256,320},{320,384},{384,448},... | collective-permute-start | bytes 196616 | tf_op jit(solution)/shard_map/ppermute | solution.py:12
  6.9 0.0 copy-start.4
  6.9 1.4 collective-permute-start.1
  8.3 0.4 collective-permute-done
  8.8 0.0 copy-start.5
  8.8 0.0 copy-done.2
  8.8 0.6 constant_dynamic-update-slice_fusion.1
  9.4 4.1 %collective-permute-done.1 = f32[16,1,8,128]{3,0,2,1:T(8,128)S(1)} collective-permute-done((f32[16,1,8,128]{3,0,2,1:T(8,128)S(1)}, f32[16,1,8,128]{3,0,2,1:T(8,128)S(1)}, u32[]{:S(2)}, u32[]{:S(2)}) %collective-permute-start.1) | collective-permute-done | bytes 65568 | tf_op jit(solution)/shard_map/ppermute | solution.py:15
  13.5 0.0 copy-start.6
  13.6 0.0 copy-done.1
  13.6 0.0 copy-done.5
  13.6 3.5 %collective-permute-start.2 = (f32[16,18,1,128]{3,0,2,1:T(8,128)S(1)}, f32[16,18,1,128]{3,0,2,1:T(8,128)S(1)}, u32[]{:S(2)}, u32[]{:S(2)}) collective-permute-start(f32[16,18,1,128]{3,0,2,1:T(8,128)S(1)} %get-tuple-element.6), channel_id=1, source_target_pairs={{0,8},{8,16},{16,24},{24,32},{32,40},{40,48},{48,56},{1,9},{9,17},... | collective-permute-start | bytes 442376 | tf_op jit(solution)/shard_map/ppermute | solution.py:12
  17.1 0.0 copy-done.6
  17.1 1.3 collective-permute-start.3
  18.4 0.0 copy-done.4
  18.4 1.1 bitcast_convert_fusion.25
  19.5 0.3 collective-permute-done.2
  19.8 4.4 %collective-permute-done.3 = f32[16,18,1,128]{3,0,2,1:T(8,128)S(1)} collective-permute-done((f32[16,18,1,128]{3,0,2,1:T(8,128)S(1)}, f32[16,18,1,128]{3,0,2,1:T(8,128)S(1)}, u32[]{:S(2)}, u32[]{:S(2)}) %collective-permute-start.3) | collective-permute-done | bytes 147488 | tf_op jit(solution)/shard_map/ppermute | solution.py:15
  24.2 0.1 pad_maximum_fusion.1
  24.3 2.1 fusion.49
  26.4 2.4 copy.12
  28.8 2.0 collective-permute-start.4
  30.9 2.4 copy.14
  33.3 3.6 %collective-permute-start.5 = (f32[16,18,10,1]{1,0,3,2:T(8,128)S(1)}, f32[16,18,10,1]{1,0,3,2:T(8,128)S(1)}, u32[]{:S(2)}, u32[]{:S(2)}) collective-permute-start(f32[16,18,10,1]{1,0,3,2:T(8,128)S(1)} %copy.14), channel_id=1, source_target_pairs={{1,0},{2,1},{3,2},{4,3},{5,4},{6,5},{7,6},{9,8},{10,9},{11,10},{12... | collective-permute-start | bytes 34568 | tf_op jit(solution)/shard_map/ppermute | solution.py:15
  37.0 0.8 bitcast_convert_fusion.24
  37.8 0.0 copy-done.7
  37.8 0.6 convert_element_type.55
  38.4 0.0 collective-permute-done.4
  38.4 2.5 copy.13
  40.9 0.0 collective-permute-done.5
  40.9 2.6 copy.15
  43.5 0.0 copy-done.3
  43.5 2.8 %maximum_maximum_fusion = (f32[16,18,10,129]{3,0,2,1:T(8,128)S(1)}, f32[16,18,10,129]{3,0,2,1:T(8,128)S(1)}) fusion(f32[16,18,1,128]{3,0,2,1:T(8,128)S(1)} %collective-permute-done.3, f32[16,18,8,128]{3,0,2,1:T(8,128)S(1)} %constant_dynamic-update-slice_fusion, f32[16,18,1,128]{3,0,2,1:T(8,128)S(1)} %collective-permute-done.2, f32[16,18,10,1]{3,0,2,1:T(8,128)} %copy.13, ...), kind=kLoop, calls=%fused_computation.2 | loop fusion | flops 2229120 | bytes 4469760 | tf_op jit(solution)/shard_map/concatenate | solution.py:16
  46.3 7.0 %fusion.16 = f32[16,16,8,128]{3,0,2,1:T(8,128)S(1)} fusion(f32[16,18,8,128]{3,0,2,1:T(8,128)S(1)} %constant_dynamic-update-slice_fusion, f32[16,18,1,128]{3,0,2,1:T(8,128)} %copy-done.3, f32[16,18,1,128]{3,0,2,1:T(8,128)S(1)} %collective-permute-done.2, f32[16,18,10,129]{3,0,2,1:T(8,128)S(1)} %get-tuple-element.3, ...), kind=kLoop, calls=%fused_computation.31 | loop fusion | flops 15990784 | bytes 24346624 | tf_op jit(solution)/shard_map/add | solution.py:37
  53.2 0.0 copy-start
  53.3 1.3 copy.18
  54.6 0.0 copy-done
  54.6 1.7 fusion.3
  56.3 102.7 %psum.14 = f32[32,16]{0,1:T(8,128)S(1)} all-reduce(f32[32,16]{0,1:T(8,128)S(1)} %fusion.3), channel_id=1, replica_groups=mesh['gx'=8,'gy'=8,'gz'=8] {'gx','gy','gz'}, use_global_device_ids=true, to_apply=%region_0.0 | all-reduce | flops 512 | bytes 4096 | tf_op jit(solution)/shard_map/psum | solution.py:53
  159.0 2.7 %convolution_subtract_fusion.1 = f32[16,16384]{1,0:T(8,128)S(1)} fusion(f32[32,16]{0,1:T(8,128)S(1)} %psum.14, f32[2,8,128,128]{3,2,1,0:T(8,128)} %bitcast.114, bf16[4,8,128,128]{3,2,1,0:T(8,128)(2,1)S(1)} %bitcast.111), kind=kOutput, calls=%fused_computation.1 | convolution fusion | flops 100925440 | bytes 3147776 | tf_op jit(solution)/shard_map/dot_general | solution.py:54
  161.7 1.7 fusion.1
  163.4 95.3 %psum.15 = f32[32,16]{0,1:T(8,128)S(1)} all-reduce(f32[32,16]{0,1:T(8,128)S(1)} %fusion.1), channel_id=1, replica_groups=mesh['gx'=8,'gy'=8,'gz'=8] {'gx','gy','gz'}, use_global_device_ids=true, to_apply=%region_1.0 | all-reduce | flops 512 | bytes 4096 | tf_op jit(solution)/shard_map/psum | solution.py:60
  258.7 0.6 add.111
  259.3 1.0 fusion
  260.3 1.2 copy.23
  (6 shorter events, 0.0 us)
Async XLA Ops:
  0.6 8.2 %copy-start.2 = (f32[16,16,8,128]{3,2,1,0:T(8,128)S(1)}, f32[16,16,8,128]{3,2,1,0:T(8,128)}, u32[]{:S(2)}) copy-start(f32[16,16,8,128]{3,2,1,0:T(8,128)} %param.5) | copy-start | bytes 3145732
  2.6 11.0 %copy-start.1 = (f32[16,16,8,128]{3,0,2,1:T(8,128)}, f32[16,16,8,128]{3,0,2,1:T(8,128)S(1)}, u32[]{:S(2)}) copy-start(f32[16,16,8,128]{3,0,2,1:T(8,128)S(1)} %copy.8) | copy-start | bytes 3145732
  2.6 6.2 %collective-permute-start = (f32[16,1,8,128]{3,0,2,1:T(8,128)S(1)}, f32[16,1,8,128]{3,0,2,1:T(8,128)S(1)}, u32[]{:S(2)}, u32[]{:S(2)}) collective-permute-start(f32[16,1,8,128]{3,0,2,1:T(8,128)S(1)} %get-tuple-element.9), channel_id=1, source_target_pairs={{0,64},{64,128},{128,192},{192,256},{256,320},{320,384},{384,448},... | collective-permute-start | bytes 196616 | tf_op jit(solution)/shard_map/ppermute | solution.py:12
  6.9 11.5 %copy-start.4 = (bf16[26,16,8,128]{3,2,1,0:T(8,128)(2,1)S(1)}, bf16[26,16,8,128]{3,2,1,0:T(8,128)(2,1)}, u32[]{:S(2)}) copy-start(bf16[26,16,8,128]{3,2,1,0:T(8,128)(2,1)} %param.7) | copy-start | bytes 2555908
  6.9 6.7 %collective-permute-start.1 = (f32[16,1,8,128]{3,0,2,1:T(8,128)S(1)}, f32[16,1,8,128]{3,0,2,1:T(8,128)S(1)}, u32[]{:S(2)}, u32[]{:S(2)}) collective-permute-start(f32[16,1,8,128]{3,0,2,1:T(8,128)S(1)} %get-tuple-element.8), channel_id=1, source_target_pairs={{64,0},{128,64},{192,128},{256,192},{320,256},{384,320},{448,384},... | collective-permute-start | bytes 196616 | tf_op jit(solution)/shard_map/ppermute | solution.py:15
  8.8 4.8 %copy-start.5 = (f32[16,1,8,128]{3,0,2,1:T(8,128)}, f32[16,1,8,128]{3,0,2,1:T(8,128)S(1)}, u32[]{:S(2)}) copy-start(f32[16,1,8,128]{3,0,2,1:T(8,128)S(1)} %collective-permute-done) | copy-start | bytes 196612
  13.5 3.6 %copy-start.6 = (f32[16,1,8,128]{3,0,2,1:T(8,128)}, f32[16,1,8,128]{3,0,2,1:T(8,128)S(1)}, u32[]{:S(2)}) copy-start(f32[16,1,8,128]{3,0,2,1:T(8,128)S(1)} %collective-permute-done.1) | copy-start | bytes 196612
  13.6 6.1 %collective-permute-start.2 = (f32[16,18,1,128]{3,0,2,1:T(8,128)S(1)}, f32[16,18,1,128]{3,0,2,1:T(8,128)S(1)}, u32[]{:S(2)}, u32[]{:S(2)}) collective-permute-start(f32[16,18,1,128]{3,0,2,1:T(8,128)S(1)} %get-tuple-element.6), channel_id=1, source_target_pairs={{0,8},{8,16},{16,24},{24,32},{32,40},{40,48},{48,56},{1,9},{9,17},... | collective-permute-start | bytes 442376 | tf_op jit(solution)/shard_map/ppermute | solution.py:12
  17.1 7.0 %collective-permute-start.3 = (f32[16,18,1,128]{3,0,2,1:T(8,128)S(1)}, f32[16,18,1,128]{3,0,2,1:T(8,128)S(1)}, u32[]{:S(2)}, u32[]{:S(2)}) collective-permute-start(f32[16,18,1,128]{3,0,2,1:T(8,128)S(1)} %get-tuple-element.7), channel_id=1, source_target_pairs={{8,0},{16,8},{24,16},{32,24},{40,32},{48,40},{56,48},{9,1},{17,9},... | collective-permute-start | bytes 442376 | tf_op jit(solution)/shard_map/ppermute | solution.py:15
  24.2 19.3 %copy-start.3 = (f32[16,18,1,128]{3,0,2,1:T(8,128)}, f32[16,18,1,128]{3,0,2,1:T(8,128)S(1)}, u32[]{:S(2)}) copy-start(f32[16,18,1,128]{3,0,2,1:T(8,128)S(1)} %collective-permute-done.3) | copy-start | bytes 442372
  28.8 8.9 %copy-start.7 = (bf16[16,8,128]{2,1,0:T(8,128)(2,1)S(1)}, bf16[16,8,128]{2,1,0:T(8,128)(2,1)}, u32[]{:S(2)}) copy-start(bf16[16,8,128]{2,1,0:T(8,128)(2,1)} %param.6) | copy-start | bytes 98308
  28.8 9.6 %collective-permute-start.4 = (f32[16,18,10,1]{1,0,3,2:T(8,128)S(1)}, f32[16,18,10,1]{1,0,3,2:T(8,128)S(1)}, u32[]{:S(2)}, u32[]{:S(2)}) collective-permute-start(f32[16,18,10,1]{1,0,3,2:T(8,128)S(1)} %copy.12), channel_id=1, source_target_pairs={{0,1},{1,2},{2,3},{3,4},{4,5},{5,6},{6,7},{8,9},{9,10},{10,11},{11... | collective-permute-start | bytes 34568 | tf_op jit(solution)/shard_map/ppermute | solution.py:12
  33.3 7.6 %collective-permute-start.5 = (f32[16,18,10,1]{1,0,3,2:T(8,128)S(1)}, f32[16,18,10,1]{1,0,3,2:T(8,128)S(1)}, u32[]{:S(2)}, u32[]{:S(2)}) collective-permute-start(f32[16,18,10,1]{1,0,3,2:T(8,128)S(1)} %copy.14), channel_id=1, source_target_pairs={{1,0},{2,1},{3,2},{4,3},{5,4},{6,5},{7,6},{9,8},{10,9},{11,10},{12... | collective-permute-start | bytes 34568 | tf_op jit(solution)/shard_map/ppermute | solution.py:15
  53.2 1.3 copy-start
where the time goes:
time: 262 us; the launch traced here: 261 us
  blocking collectives  198 us (76%)
  local copies, waits for them, and re-layouts  17.2 us (7%)
  starting transfers between devices  16.2 us (6%)
  other arithmetic  13 us (5%)
  waiting for transfers between devices  9.25 us (4%)
  matrix products  7.09 us (3%)
    psum x1, blocking collectives, local(): first = lax.psum(local_first, ('gx', 'gy', 'gz'))  103 us
    psum x1, blocking collectives, local(): second = lax.psum(local_second, ('gx', 'gy', 'gz'))  95.3 us
    ppermute x3, starting transfers between devices, extended(): lax.ppermute(lax.slice_in_dim(block, block.shape[dim] - width, None, axis...  9.81 us
    ppermute x3, waiting for transfers between devices, extended(): lax.ppermute(lax.slice_in_dim(block, 0, width, axis=dim), axis, backward)  8.55 us
    add x1, other arithmetic, local(): image = image + couplings[which].astype(jnp.float32)[None] * moved  6.97 us
    ppermute x3, starting transfers between devices, extended(): lax.ppermute(lax.slice_in_dim(block, 0, width, axis=dim), axis, backward)  6.35 us
  transfers between devices with their start and end apart: 6, of which 4 were waited for; matrix products, arithmetic and copies ran while one was open for 3% of the time, Pallas kernels for 0%

commit v1 on v0

--- a/solution.py
+++ b/solution.py
@@ -15,6 +15,14 @@
         high = lax.ppermute(lax.slice_in_dim(block, 0, width, axis=dim), axis, backward)
         block = jnp.concatenate([low, block, high], axis=dim)
     return block
+
+
+def summed(values, axes):
+    count = 1
+    for axis in axes:
+        count *= lax.axis_size(axis)
+    copies = jnp.broadcast_to(values[None], (count,) + values.shape)
+    return lax.all_to_all(copies, axes, 0, 0).sum(0)
 
 
 def local(basis, krylov, center, couplings):
@@ -43,25 +51,21 @@
     flat_basis = basis.reshape(count_u, -1)
     flat_image = image.reshape(count_v, -1)
     dims = (((1,), (1,)), ((), ()))
-    local_first = scale * lax.dot_general(
-        flat_basis,
-        flat_image,
-        dims,
-        precision=lax.Precision.HIGHEST,
-        preferred_element_type=jnp.float32,
+    high = lax.Precision.HIGHEST
+    gram = lax.dot_general(flat_basis, flat_basis, dims, preferred_element_type=jnp.float32)
+    part = lax.dot_general(
+        flat_basis, flat_image, dims, precision=high, preferred_element_type=jnp.float32
     )
-    first = lax.psum(local_first, ("gx", "gy", "gz"))
-    once = flat_image - jnp.dot(
-        first.T, flat_basis, precision=lax.Precision.HIGHEST, preferred_element_type=jnp.float32
+    payload = (scale * jnp.concatenate([gram, part], axis=1)).reshape(-1, 128)
+    payload = summed(payload, ("gz",))
+    payload = summed(payload, ("gx", "gy"))
+    payload = payload.reshape(count_u, count_u + count_v)
+    gram, first = payload[:, :count_u], payload[:, count_u:]
+    coefficients = first + (first - jnp.dot(gram, first, precision=high))
+    projected = flat_image - jnp.dot(
+        coefficients.T, flat_basis, precision=high, preferred_element_type=jnp.float32
     )
-    local_second = scale * lax.dot_general(
-        flat_basis, once, dims, precision=lax.Precision.HIGHEST, preferred_element_type=jnp.float32
-    )
-    second = lax.psum(local_second, ("gx", "gy", "gz"))
-    projected = once - jnp.dot(
-        second.T, flat_basis, precision=lax.Precision.HIGHEST, preferred_element_type=jnp.float32
-    )
-    return (projected.reshape(count_v, size_x, size_y, size_z), first + second)
+    return (projected.reshape(count_v, size_x, size_y, size_z), coefficients)
 
 
 def solution(mesh):

time: 262 us -> 107 us (0.41)
  the two profiles are of different devices: /device:TPU:2 before, /device:TPU:8 now
where the time goes in v1:
time: 107 us; the launch traced here: 106 us
  starting transfers between devices  30.1 us (28%)
  waiting for transfers between devices  26.1 us (24%)
  local copies, waits for them, and re-layouts  17.5 us (16%)
  other arithmetic  13.5 us (13%)
  blocking collectives  12.7 us (12%)
  matrix products  5.44 us (5%)
    all_to_all x1, waiting for transfers between devices, summed(): return lax.all_to_all(copies, axes, 0, 0).sum(0)  18.8 us
    all_to_all x1, starting transfers between devices, summed(): return lax.all_to_all(copies, axes, 0, 0).sum(0)  16 us
    all_to_all x1, blocking collectives, summed(): return lax.all_to_all(copies, axes, 0, 0).sum(0)  12.7 us
    ppermute x3, starting transfers between devices, extended(): lax.ppermute(lax.slice_in_dim(block, block.shape[dim] - width, None, axis...  9.18 us
    ppermute x3, waiting for transfers between devices, extended(): lax.ppermute(lax.slice_in_dim(block, 0, width, axis=dim), axis, backward)  6.96 us
    add x1, other arithmetic, local(): image = image + couplings[which].astype(jnp.float32)[None] * moved  6.85 us
    ppermute x3, starting transfers between devices, extended(): lax.ppermute(lax.slice_in_dim(block, 0, width, axis=dim), axis, backward)  4.94 us
    slice x3, local copies, waits for them, and re-layouts, extended(): lax.slice_in_dim(block, block.shape[dim] - width, None, axis=dim)  4.63 us
  transfers between devices with their start and end apart: 7, of which 4 were waited for; matrix products, arithmetic and copies ran while one was open for 9% of the time, Pallas kernels for 0%

profile of v1, /device:TPU:8, one launch (start us, length us, event | category | flops | bytes accessed | tf_op | source)
XLA Modules:
  0.0 106.2 jit_solution(9338260418369654508)
XLA Ops:
  0.6 1.9 %copy.49 = f32[16,16,8,128]{3,0,2,1:T(8,128)S(1)} copy(f32[16,16,8,128]{3,2,1,0:T(8,128)} %param.5) | data formatting | bytes 2097152 | tf_op args[1]
  2.6 0.0 copy-start
  2.6 0.0 copy-start.3
  2.6 4.4 %collective-permute-start = (f32[16,1,8,128]{3,0,2,1:T(8,128)S(1)}, f32[16,1,8,128]{3,0,2,1:T(8,128)S(1)}, u32[]{:S(2)}, u32[]{:S(2)}) collective-permute-start(f32[16,1,8,128]{3,0,2,1:T(8,128)S(1)} %get-tuple-element.9), channel_id=1, source_target_pairs={{0,64},{64,128},{128,192},{192,256},{256,320},{320,384},{384,448},... | collective-permute-start | bytes 196616 | tf_op jit(solution)/shard_map/ppermute | solution.py:12
  7.0 1.3 %collective-permute-start.1 = (f32[16,1,8,128]{3,0,2,1:T(8,128)S(1)}, f32[16,1,8,128]{3,0,2,1:T(8,128)S(1)}, u32[]{:S(2)}, u32[]{:S(2)}) collective-permute-start(f32[16,1,8,128]{3,0,2,1:T(8,128)S(1)} %get-tuple-element.8), channel_id=1, source_target_pairs={{64,0},{128,64},{192,128},{256,192},{320,256},{384,320},{448,384},... | collective-permute-start | bytes 196616 | tf_op jit(solution)/shard_map/ppermute | solution.py:15
  8.3 1.1 %bitcast_convert_fusion.25 = (f32[16,8,128]{2,1,0:T(8,128)}, f32[16,8,128]{2,1,0:T(8,128)}, f32[16,8,128]{2,1,0:T(8,128)}, f32[16,8,128]{2,1,0:T(8,128)}, f32[16...) fusion(bf16[26,16,8,128]{3,2,1,0:T(8,128)(2,1)S(1)} %copy-done.5), kind=kLoop, calls=%fused_computation.106 | loop fusion | flops 311296 | bytes 1867776 | tf_op jit(solution)/shard_map/mul | solution.py:45
  9.4 0.0 collective-permute-done
  9.5 0.6 constant_dynamic-update-slice_fusion.1
  10.1 3.5 %collective-permute-done.1 = f32[16,1,8,128]{3,0,2,1:T(8,128)S(1)} collective-permute-done((f32[16,1,8,128]{3,0,2,1:T(8,128)S(1)}, f32[16,1,8,128]{3,0,2,1:T(8,128)S(1)}, u32[]{:S(2)}, u32[]{:S(2)}) %collective-permute-start.1) | collective-permute-done | bytes 65568 | tf_op jit(solution)/shard_map/ppermute | solution.py:15
  13.6 0.0 copy-done.6
  13.6 3.5 %collective-permute-start.2 = (f32[16,18,1,128]{3,0,2,1:T(8,128)S(1)}, f32[16,18,1,128]{3,0,2,1:T(8,128)S(1)}, u32[]{:S(2)}, u32[]{:S(2)}) collective-permute-start(f32[16,18,1,128]{3,0,2,1:T(8,128)S(1)} %get-tuple-element.6), channel_id=1, source_target_pairs={{0,8},{8,16},{16,24},{24,32},{32,40},{40,48},{48,56},{1,9},{9,17},... | collective-permute-start | bytes 442376 | tf_op jit(solution)/shard_map/ppermute | solution.py:12
  17.1 2.4 %collective-permute-start.3 = (f32[16,18,1,128]{3,0,2,1:T(8,128)S(1)}, f32[16,18,1,128]{3,0,2,1:T(8,128)S(1)}, u32[]{:S(2)}, u32[]{:S(2)}) collective-permute-start(f32[16,18,1,128]{3,0,2,1:T(8,128)S(1)} %get-tuple-element.7), channel_id=1, source_target_pairs={{8,0},{16,8},{24,16},{32,24},{40,32},{48,40},{56,48},{9,1},{17,9},... | collective-permute-start | bytes 442376 | tf_op jit(solution)/shard_map/ppermute | solution.py:15
  19.5 0.8 bitcast_convert_fusion.24
  20.2 0.4 collective-permute-done.2
  20.6 3.5 %collective-permute-done.3 = f32[16,18,1,128]{3,0,2,1:T(8,128)S(1)} collective-permute-done((f32[16,18,1,128]{3,0,2,1:T(8,128)S(1)}, f32[16,18,1,128]{3,0,2,1:T(8,128)S(1)}, u32[]{:S(2)}, u32[]{:S(2)}) %collective-permute-start.3) | collective-permute-done | bytes 147488 | tf_op jit(solution)/shard_map/ppermute | solution.py:15
  24.1 0.1 pad_maximum_fusion.1
  24.3 2.1 %fusion.46 = (f32[16,18,10,1]{3,0,2,1:T(8,128)}, f32[16,18,10,1]{3,0,2,1:T(8,128)}) fusion(f32[16,18,10,128]{3,0,2,1:T(8,128)S(1)} %pad_maximum_fusion.1), kind=kLoop, calls=%fused_computation.113 | loop fusion | bytes 46080 | tf_op jit(solution)/shard_map/slice | solution.py:13
  26.3 2.5 %copy.53 = f32[16,18,10,1]{1,0,3,2:T(8,128)S(1)} copy(f32[16,18,10,1]{3,0,2,1:T(8,128)} %get-tuple-element.4) | data formatting | bytes 23040 | tf_op jit(solution)/shard_map/slice | solution.py:13
  28.9 1.3 %collective-permute-start.4 = (f32[16,18,10,1]{1,0,3,2:T(8,128)S(1)}, f32[16,18,10,1]{1,0,3,2:T(8,128)S(1)}, u32[]{:S(2)}, u32[]{:S(2)}) collective-permute-start(f32[16,18,10,1]{1,0,3,2:T(8,128)S(1)} %copy.53), channel_id=1, source_target_pairs={{0,1},{1,2},{2,3},{3,4},{4,5},{5,6},{6,7},{8,9},{9,10},{10,11},{11... | collective-permute-start | bytes 34568 | tf_op jit(solution)/shard_map/ppermute | solution.py:12
  30.2 0.0 copy-start.9
  30.2 2.4 %copy.55 = f32[16,18,10,1]{1,0,3,2:T(8,128)S(1)} copy(f32[16,18,10,1]{3,0,2,1:T(8,128)} %get-tuple-element.5) | data formatting | bytes 23040 | tf_op jit(solution)/shard_map/slice | solution.py:15
  32.6 1.3 %collective-permute-start.5 = (f32[16,18,10,1]{1,0,3,2:T(8,128)S(1)}, f32[16,18,10,1]{1,0,3,2:T(8,128)S(1)}, u32[]{:S(2)}, u32[]{:S(2)}) collective-permute-start(f32[16,18,10,1]{1,0,3,2:T(8,128)S(1)} %copy.55), channel_id=1, source_target_pairs={{1,0},{2,1},{3,2},{4,3},{5,4},{6,5},{7,6},{9,8},{10,9},{11,10},{12... | collective-permute-start | bytes 34568 | tf_op jit(solution)/shard_map/ppermute | solution.py:15
  33.9 0.7 convolution_bitcast_fusion.1
  34.7 0.0 copy-done.9
  34.7 0.6 convert_element_type.55
  35.3 0.0 collective-permute-done.4
  35.3 2.6 %copy.54 = f32[16,18,10,1]{3,0,2,1:T(8,128)} copy(f32[16,18,10,1]{1,0,3,2:T(8,128)S(1)} %collective-permute-done.4) | data formatting | bytes 23040 | tf_op jit(solution)/shard_map/ppermute | solution.py:12
  37.9 0.0 collective-permute-done.5
  37.9 2.6 %copy.56 = f32[16,18,10,1]{3,0,2,1:T(8,128)} copy(f32[16,18,10,1]{1,0,3,2:T(8,128)S(1)} %collective-permute-done.5) | data formatting | bytes 23040 | tf_op jit(solution)/shard_map/ppermute | solution.py:15
  40.4 2.8 %maximum_maximum_fusion = (f32[16,18,10,129]{3,0,2,1:T(8,128)S(1)}, f32[16,18,10,129]{3,0,2,1:T(8,128)S(1)}) fusion(f32[16,18,1,128]{3,0,2,1:T(8,128)S(1)} %collective-permute-done.3, f32[16,18,8,128]{3,0,2,1:T(8,128)S(1)} %constant_dynamic-update-slice_fusion, f32[16,18,1,128]{3,0,2,1:T(8,128)S(1)} %collective-permute-done.2, f32[16,18,10,1]{3,0,2,1:T(8,128)} %copy.54, ...), kind=kLoop, calls=%fused_computation.1 | loop fusion | flops 2229120 | bytes 4469760 | tf_op jit(solution)/shard_map/concatenate | solution.py:16
  43.2 6.9 %fusion.14 = f32[16,16,8,128]{3,0,2,1:T(8,128)S(1)} fusion(f32[16,18,8,128]{3,0,2,1:T(8,128)S(1)} %constant_dynamic-update-slice_fusion, f32[16,18,1,128]{3,0,2,1:T(8,128)} %copy-done.4, f32[16,18,1,128]{3,0,2,1:T(8,128)S(1)} %collective-permute-done.2, f32[16,18,10,129]{3,0,2,1:T(8,128)S(1)} %get-tuple-element.3, ...), kind=kLoop, calls=%fused_computation.29 | loop fusion | flops 15990784 | bytes 24346624 | tf_op jit(solution)/shard_map/add | solution.py:45
  50.1 2.9 %convolution_bitcast_fusion = f32[32,16]{1,0:T(8,128)S(1)} fusion(f32[16,16,8,128]{3,0,2,1:T(8,128)S(1)} %fusion.14, bf16[32,16,8,128]{3,2,1,0:T(8,128)(2,1)} %param.4), kind=kOutput, calls=%fused_computation.13 | convolution fusion | flops 100663296 | bytes 2099200 | tf_op jit(solution)/shard_map/dot_general | solution.py:56
  53.0 0.1 maximum_multiply_fusion
  53.1 0.1 mul.467
  53.2 12.7 %all_to_all.10 = f32[8,12,128]{2,1,0:T(8,128)S(1)} all-to-all(f32[8,12,128]{2,1,0:T(8,128)S(1)} %broadcast_in_dim.4), channel_id=1, replica_groups=mesh['gx'=8,'gy'=8,'gz'=8] {'gz'}, dimensions={0} | all-to-all | bytes 98304 | tf_op jit(solution)/shard_map/all_to_all | solution.py:25
  65.9 0.8 broadcast_in_dim.5
  66.8 16.0 %all-to-all-start.1 = ((f32[64,12,128]{2,1,0:T(8,128)}), f32[64,12,128]{2,1,0:T(8,128)}, u32[]{:S(2)}, u32[]{:S(2)}) async-start(f32[64,12,128]{2,1,0:T(8,128)} %broadcast_in_dim.5), calls=%async_computation.1 | async-start | bytes 1048576 | tf_op jit(solution)/shard_map/all_to_all | solution.py:25
  82.7 0.0 copy-start.2
  82.8 0.3 copy.59
  83.1 18.8 %all-to-all-done.1 = f32[64,12,128]{2,1,0:T(8,128)} async-done(((f32[64,12,128]{2,1,0:T(8,128)}), f32[64,12,128]{2,1,0:T(8,128)}, u32[]{:S(2)}, u32[]{:S(2)}) %all-to-all-start.1) | async-done | bytes 393248 | tf_op jit(solution)/shard_map/all_to_all | solution.py:25
  101.9 1.1 %reduce_sum.19 = f32[12,128]{1,0:T(8,128)S(1)} reduce(f32[64,12,128]{2,1,0:T(8,128)} %all-to-all-done.1, f32[]{:T(128)} %constant.1.clone.1), dimensions={0}, to_apply=%region_1.0 | reduce | flops 96768 | bytes 399364 | tf_op jit(solution)/shard_map/reduce_sum | solution.py:25
  103.0 0.1 reshape.26
  103.1 0.1 slice.298
  103.2 0.1 copy.72
  103.2 0.3 fusion.1
  103.5 0.0 copy-start.8
  103.5 1.5 %fusion = f32[2,8,128,128]{3,1,2,0:T(8,128)S(1)} fusion(f32[32,16]{0,1:T(8,128)S(1)} %fusion.1, bf16[4,8,128,128]{3,2,1,0:T(8,128)(2,1)S(1)} %bitcast.101, f32[2,8,128,128]{3,2,1,0:T(8,128)S(1)} %bitcast.102), kind=kOutput, calls=%fused_computation.8 | convolution fusion | flops 100925440 | bytes 3147776 | tf_op jit(solution)/shard_map/dot_general | solution.py:65
  105.0 1.2 %copy.75 = f32[2,8,128,128]{3,2,1,0:T(8,128)} copy(f32[2,8,128,128]{3,1,2,0:T(8,128)S(1)} %fusion) | data formatting | bytes 2097152
  (19 shorter events, 0.1 us)
Async XLA Ops:
  0.6 7.7 %copy-start.5 = (bf16[26,16,8,128]{3,2,1,0:T(8,128)(2,1)S(1)}, bf16[26,16,8,128]{3,2,1,0:T(8,128)(2,1)}, u32[]{:S(2)}) copy-start(bf16[26,16,8,128]{3,2,1,0:T(8,128)(2,1)} %param.7) | copy-start | bytes 2555908
  2.6 7.5 %copy-start = (f32[16,16,8,128]{3,0,2,1:T(8,128)}, f32[16,16,8,128]{3,0,2,1:T(8,128)S(1)}, u32[]{:S(2)}) copy-start(f32[16,16,8,128]{3,0,2,1:T(8,128)S(1)} %copy.49) | copy-start | bytes 3145732
  2.6 6.9 %copy-start.3 = (f32[16,16,8,128]{3,2,1,0:T(8,128)S(1)}, f32[16,16,8,128]{3,2,1,0:T(8,128)}, u32[]{:S(2)}) copy-start(f32[16,16,8,128]{3,2,1,0:T(8,128)} %param.5) | copy-start | bytes 3145732
  2.6 6.8 %collective-permute-start = (f32[16,1,8,128]{3,0,2,1:T(8,128)S(1)}, f32[16,1,8,128]{3,0,2,1:T(8,128)S(1)}, u32[]{:S(2)}, u32[]{:S(2)}) collective-permute-start(f32[16,1,8,128]{3,0,2,1:T(8,128)S(1)} %get-tuple-element.9), channel_id=1, source_target_pairs={{0,64},{64,128},{128,192},{192,256},{256,320},{320,384},{384,448},... | collective-permute-start | bytes 196616 | tf_op jit(solution)/shard_map/ppermute | solution.py:12
  7.0 6.5 %collective-permute-start.1 = (f32[16,1,8,128]{3,0,2,1:T(8,128)S(1)}, f32[16,1,8,128]{3,0,2,1:T(8,128)S(1)}, u32[]{:S(2)}, u32[]{:S(2)}) collective-permute-start(f32[16,1,8,128]{3,0,2,1:T(8,128)S(1)} %get-tuple-element.8), channel_id=1, source_target_pairs={{64,0},{128,64},{192,128},{256,192},{320,256},{384,320},{448,384},... | collective-permute-start | bytes 196616 | tf_op jit(solution)/shard_map/ppermute | solution.py:15
  9.4 4.2 %copy-start.6 = (f32[16,1,8,128]{3,0,2,1:T(8,128)}, f32[16,1,8,128]{3,0,2,1:T(8,128)S(1)}, u32[]{:S(2)}) copy-start(f32[16,1,8,128]{3,0,2,1:T(8,128)S(1)} %collective-permute-done) | copy-start | bytes 196612
  13.5 3.5 %copy-start.7 = (f32[16,1,8,128]{3,0,2,1:T(8,128)}, f32[16,1,8,128]{3,0,2,1:T(8,128)S(1)}, u32[]{:S(2)}) copy-start(f32[16,1,8,128]{3,0,2,1:T(8,128)S(1)} %collective-permute-done.1) | copy-start | bytes 196612
  13.6 7.0 %collective-permute-start.2 = (f32[16,18,1,128]{3,0,2,1:T(8,128)S(1)}, f32[16,18,1,128]{3,0,2,1:T(8,128)S(1)}, u32[]{:S(2)}, u32[]{:S(2)}) collective-permute-start(f32[16,18,1,128]{3,0,2,1:T(8,128)S(1)} %get-tuple-element.6), channel_id=1, source_target_pairs={{0,8},{8,16},{16,24},{24,32},{32,40},{40,48},{48,56},{1,9},{9,17},... | collective-permute-start | bytes 442376 | tf_op jit(solution)/shard_map/ppermute | solution.py:12
  17.1 7.0 %collective-permute-start.3 = (f32[16,18,1,128]{3,0,2,1:T(8,128)S(1)}, f32[16,18,1,128]{3,0,2,1:T(8,128)S(1)}, u32[]{:S(2)}, u32[]{:S(2)}) collective-permute-start(f32[16,18,1,128]{3,0,2,1:T(8,128)S(1)} %get-tuple-element.7), channel_id=1, source_target_pairs={{8,0},{16,8},{24,16},{32,24},{40,32},{48,40},{56,48},{9,1},{17,9},... | collective-permute-start | bytes 442376 | tf_op jit(solution)/shard_map/ppermute | solution.py:15
  24.1 16.3 %copy-start.4 = (f32[16,18,1,128]{3,0,2,1:T(8,128)}, f32[16,18,1,128]{3,0,2,1:T(8,128)S(1)}, u32[]{:S(2)}) copy-start(f32[16,18,1,128]{3,0,2,1:T(8,128)S(1)} %collective-permute-done.3) | copy-start | bytes 442372
  26.3 7.6 %copy-start.1 = (bf16[32,16,8,128]{3,2,1,0:T(8,128)(2,1)S(1)}, bf16[32,16,8,128]{3,2,1,0:T(8,128)(2,1)}, u32[]{:S(2)}) copy-start(bf16[32,16,8,128]{3,2,1,0:T(8,128)(2,1)} %param.4) | copy-start | bytes 3145732
  28.9 6.4 %collective-permute-start.4 = (f32[16,18,10,1]{1,0,3,2:T(8,128)S(1)}, f32[16,18,10,1]{1,0,3,2:T(8,128)S(1)}, u32[]{:S(2)}, u32[]{:S(2)}) collective-permute-start(f32[16,18,10,1]{1,0,3,2:T(8,128)S(1)} %copy.53), channel_id=1, source_target_pairs={{0,1},{1,2},{2,3},{3,4},{4,5},{5,6},{6,7},{8,9},{9,10},{10,11},{11... | collective-permute-start | bytes 34568 | tf_op jit(solution)/shard_map/ppermute | solution.py:12
  30.2 4.5 %copy-start.9 = (bf16[16,8,128]{2,1,0:T(8,128)(2,1)S(1)}, bf16[16,8,128]{2,1,0:T(8,128)(2,1)}, u32[]{:S(2)}) copy-start(bf16[16,8,128]{2,1,0:T(8,128)(2,1)} %param.6) | copy-start | bytes 98308
  32.6 5.3 %collective-permute-start.5 = (f32[16,18,10,1]{1,0,3,2:T(8,128)S(1)}, f32[16,18,10,1]{1,0,3,2:T(8,128)S(1)}, u32[]{:S(2)}, u32[]{:S(2)}) collective-permute-start(f32[16,18,10,1]{1,0,3,2:T(8,128)S(1)} %copy.55), channel_id=1, source_target_pairs={{1,0},{2,1},{3,2},{4,3},{5,4},{6,5},{7,6},{9,8},{10,9},{11,10},{12... | collective-permute-start | bytes 34568 | tf_op jit(solution)/shard_map/ppermute | solution.py:15
  66.8 35.1 %all-to-all-start.1 = ((f32[64,12,128]{2,1,0:T(8,128)}), f32[64,12,128]{2,1,0:T(8,128)}, u32[]{:S(2)}, u32[]{:S(2)}) async-start(f32[64,12,128]{2,1,0:T(8,128)} %broadcast_in_dim.5), calls=%async_computation.1 | async-start | bytes 1048576 | tf_op jit(solution)/shard_map/all_to_all | solution.py:25
  82.7 20.8 %copy-start.2 = (bf16[32,16,8,128]{3,2,1,0:T(8,128)(2,1)S(1)}, bf16[32,16,8,128]{3,2,1,0:T(8,128)(2,1)}, u32[]{:S(2)}) copy-start(bf16[32,16,8,128]{3,2,1,0:T(8,128)(2,1)} %param.4) | copy-start | bytes 3145732
  103.5 1.5 %copy-start.8 = (f32[32,16]{0,1:T(8,128)}, f32[32,16]{0,1:T(8,128)S(1)}, u32[]{:S(2)}) copy-start(f32[32,16]{0,1:T(8,128)S(1)} %fusion.1) | copy-start | bytes 6148

commit v2 on v0

v2 whole, which is shorter than its diff:
```python
import jax
import jax.numpy as jnp
import numpy as np
from jax import lax
from jax.experimental import pallas as pl
from jax.experimental.pallas import tpu as pltpu
from jax.sharding import PartitionSpec as P

F32 = jnp.float32
BF16 = jnp.bfloat16
NT = (((1,), (1,)), ((), ()))
STEPS = (-1, 0, 1)


def call(name, body, out, scratch=(), flops=0, data=0, aliases=None):
    single = not isinstance(out, (tuple, list))
    shapes = (out,) if single else tuple(out)
    built = pl.pallas_call(
        body,
        name=name,
        out_shape=shapes[0] if single else shapes,
        scratch_shapes=list(scratch),
        input_output_aliases=aliases or {},
        compiler_params=pltpu.CompilerParams(vmem_limit_bytes=40 << 20),
        cost_estimate=pl.CostEstimate(flops=flops, bytes_accessed=data, transcendentals=0),
    )
    return built


def like(shape, dtype=F32):
    return jax.ShapeDtypeStruct(shape, dtype)


def roll(value, shift, axis):
    size = value.shape[axis]
    shift = shift % size
    return value if shift == 0 else pltpu.roll(value, shift, axis)


def lanes(shape):
    return lax.broadcasted_iota(jnp.int32, shape, len(shape) - 1)


def rows(shape):
    return lax.broadcasted_iota(jnp.int32, shape, len(shape) - 2)


def spread(terms):
    total = None
    for c in STEPS:
        part = terms[0, c] + roll(terms[-1, c], 1, 0) + roll(terms[1, c], -1, 0)
        part = roll(part, -c, 1)
        total = part if total is None else total + part
    return total


def y_faces(krylov, low, high):
    low[...] = krylov[:, :, 0, :]
    high[...] = krylov[:, :, 7, :]


def number(a, b, c):
    k = (a + 1) * 9 + (b + 1) * 3 + (c + 1)
    return k if k < 13 else k - 1


def interior(krylov, center, couplings, image, z_high, z_low, face_x, face_y, face_z, weights, flat):
    lane = lanes((8, 128))
    row = rows((8, 128))
    slot = lanes((8, 128)) % 32

    def prepare(x, carry):
        edge_of = {}
        for a in STEPS:
            for b in STEPS:
                for c in STEPS:
                    index = (a + 1) * 9 + (b + 1) * 3 + (c + 1)
                    if (a, b, c) == (0, 0, 0):
                        value = center[x].astype(F32)
                    else:
                        value = couplings[number(a, b, c), x].astype(F32)
                    edge_of[a, b, c] = value
                    if c == -1:
                        value = jnp.where(lane == 0, 0.0, value)
                    if c == 1:
                        value = jnp.where(lane == 127, 0.0, value)
                    value = roll(value, c, 1)
                    if b != 0:
                        flat[(a + 1) * 6 + (b + 1) // 2 * 3 + (c + 1), x] = value
                        value = jnp.where(row == (0 if b == -1 else 7), 0.0, value)
                    value = roll(value, b, 0)
                    weights[index, x] = value
        for a in STEPS:
            for b in STEPS:
                both = jnp.where(lane == 127, edge_of[a, b, 1], edge_of[a, b, -1])
                for side, start in ((0, 0), (1, 127)):
                    moved = pltpu.roll(both, (x + 1 + 128 - start) % 128, 1)
                    k = (a + 1) * 3 + b + 1
                    face_z[side, k] = jnp.where(lane == x + 1, moved, face_z[side, k])
        return carry

    face_z[...] = jnp.zeros_like(face_z)
    lax.fori_loop(0, 16, prepare, 0)
    for side in range(2):
        for k in range(9):
            value = face_z[side, k]
            value = value + roll(value, 32, 1)
            face_z[side, k] = value + roll(value, 64, 1)
    zero = jnp.zeros((8, 128), F32)
    for k in range(9):
        face_x[0, k] = weights[k, 0]
        face_x[1, k] = weights[18 + k, 15]
        weights[k, 0] = zero
        weights[18 + k, 15] = zero
    for a in range(3):
        for c in range(3):
            face_y[0, a * 3 + c] = flat[a * 6 + c, :, 0, :]
            face_y[1, a * 3 + c] = flat[a * 6 + 3 + c, :, 7, :]

    z_high[...] = jnp.zeros_like(z_high)
    z_low[...] = jnp.zeros_like(z_low)

    def plane(x, carry):
        before = jnp.maximum(x - 1, 0)
        after = jnp.minimum(x + 1, 15)
        for group in range(4):
            high = z_high[group]
            low = z_low[group]
            for inner in range(4):
                j = group * 4 + inner
                source = {-1: krylov[j, before], 0: krylov[j, x], 1: krylov[j, after]}
                terms = {}
                for b in STEPS:
                    for c in STEPS:
                        k = (b + 1) * 3 + (c + 1)
                        terms[b, c] = (
                            weights[k, x] * source[-1]
                            + weights[9 + k, x] * source[0]
                            + weights[18 + k, x] * source[1]
                        )
                image[j, x] = spread(terms)
                place = inner * 32 + 1 + x
                here = lane == place
                high = jnp.where(here, pltpu.roll(source[0], (place + 1) % 128, 1), high)
                low = jnp.where(here, pltpu.roll(source[0], place % 128, 1), low)
            z_high[group] = high
            z_low[group] = low
        return carry

    lax.fori_loop(0, 16, plane, 0)


def x_faces(krylov, y_low, y_high, after, low, high):
    del after
    for out, x in ((low, 0), (high, 15)):
        out[0:128, :] = krylov[:, x].reshape(128, 128)
        for side, face in ((0, y_low), (1, y_high)):
            for slot in range(4):
                out[pl.ds(128 + slot * 8 + side * 4, 4), :] = face[pl.ds(slot, 4, stride=4), x, :]


def same_row():
    return (lanes((8, 256)) % 8 == rows((8, 256))).astype(F32)


def fold_rows(product):
    groups = product.shape[0] // 8
    return jnp.sum(product.reshape(groups, 8, 256) * same_row()[None], axis=1)


def fold_lanes(value):
    value = value + roll(value, 127, 1)
    value = value + roll(value, 126, 1)
    value = value + roll(value, 124, 1)
    return jnp.where(lanes(value.shape) % 8 == 0, value, 0.0)


def pack(value):
    total = None
    for group in range(value.shape[0] // 8):
        for half in range(2):
            part = fold_lanes(value[group * 8 : group * 8 + 8, half * 128 : half * 128 + 128])
            part = roll(part, group * 2 + half, 1)
            total = part if total is None else total + part
    return total


def unpack(value, groups):
    out = []
    lane = lanes(value.shape)
    for group in range(groups):
        halves = []
        for half in range(2):
            part = jnp.where(lane % 8 == 0, roll(value, -(group * 2 + half), 1), 0.0)
            part = part + roll(part, 1, 1)
            part = part + roll(part, 2, 1)
            halves.append(part + roll(part, 4, 1))
        out.append(jnp.concatenate(halves, axis=1))
    return jnp.concatenate(out, axis=0)


def basis_kernel(scale, basis, y_low, y_high, flat, gram, edge_basis, edge_y):
    for x in range(16):
        block = basis[:, x].astype(F32).reshape(256, 128)
        flat[:, x * 128 : x * 128 + 128] = block.astype(BF16)
    whole = flat[...]
    product = lax.dot_general(whole, whole, NT, preferred_element_type=F32)
    gram[...] = pack(fold_rows(product)) * scale
    row = rows((2048, 128))
    lane = lanes((2048, 128))
    x = row // 128
    z = row % 128
    chosen = jnp.where(((z == 0) & (lane == 1 + x)) | ((z == 127) & (lane == 65 + x)), 1.0, 0.0)
    edge_basis[...] = jnp.dot(
        whole, chosen.astype(BF16), preferred_element_type=F32
    ).astype(BF16)
    line = lanes((16, 128))
    columns = jnp.zeros((16, 128), F32)
    for yside, face in ((0, y_low), (1, y_high)):
        for j in range(16):
            place = (j % 4) * 8 + yside * 4 + j // 4
            columns = jnp.where(line == place, roll(face[j], place + 1, 1), columns)
            columns = jnp.where(line == 64 + place, roll(face[j], 64 + place, 1), columns)
    turned = jnp.concatenate([columns, jnp.zeros((112, 128), F32)], axis=0).T
    lane = lanes((8, 128))
    for side in range(2):
        total = jnp.zeros((8, 128), F32)
        for slot in range(4):
            part = turned[side * 64 + slot * 8 : side * 64 + slot * 8 + 8, :]
            inside = (lane >= slot * 32 + 1) & (lane < slot * 32 + 17)
            total = jnp.where(inside, roll(part, slot * 32 + 1, 1), total)
        edge_y[side] = total


def z_faces(z_high, z_low, edge_y, x_low, x_high, out_high, out_low):
    lane = lanes((8, 128))
    for side, (own, out) in enumerate(((z_high, out_high), (z_low, out_low))):
        for group in range(5):
            value = edge_y[side] if group == 4 else own[group]
            for slot in range(4):
                first = 128 + slot * 8 if group == 4 else (group * 4 + slot) * 8
                for face, q in ((x_low, 0), (x_high, 17)):
                    place = slot * 32 + q
                    part = roll(face[first : first + 8, :], place + 1 - side, 1)
                    value = jnp.where(lane == place, part, value)
            out[group * 8 : group * 8 + 8, :] = value


def corrections(y_low, y_high, x_low, x_high, face_x, face_y, flat, given, image, partial, halves):
    row = rows((16, 128))

    def vector(j, carry):
        for side, (face, x) in enumerate(((x_low, 0), (x_high, 15))):
            source = face[pl.ds(pl.multiple_of(j * 8, 8), 8), :]
            terms = {}
            for b in STEPS:
                for c in STEPS:
                    terms[b, c] = face_x[side, (b + 1) * 3 + c + 1] * source
            image[j, x] = given[j, x] + spread(terms)
        for x in range(1, 15):
            image[j, x] = given[j, x]
        corner = 128 + (j % 4) * 8 + j // 4
        for side, (face, y) in enumerate(((y_low, 0), (y_high, 7))):
            middle = face[j]
            before = jnp.where(row == 0, x_low[pl.ds(corner + side * 4, 1), :], roll(middle, 1, 0))
            after = jnp.where(row == 15, x_high[pl.ds(corner + side * 4, 1), :], roll(middle, -1, 0))
            total = None
            for c in STEPS:
                part = (
                    face_y[side, c + 1] * before
                    + face_y[side, 3 + c + 1] * middle
                    + face_y[side, 6 + c + 1] * after
                )
                part = roll(part, -c, 1)
                total = part if total is None else total + part
            image[j, :, y, :] = image[j, :, y, :] + total
        return carry

    lax.fori_loop(0, 16, vector, 0)
    for x in range(16):
        block = image[:, x].reshape(128, 128)
        upper = block.astype(BF16)
        halves[0:128, x * 128 : x * 128 + 128] = upper
        halves[128:256, x * 128 : x * 128 + 128] = (block - upper.astype(F32)).astype(BF16)
    product = lax.dot_general(halves[...], flat[...], NT, preferred_element_type=F32)
    partial[...] = fold_rows(product[0:128] + product[128:256])


def finish(scale, from_low, from_high, face_z, edge_basis, partial, gram, columns, payload):
    row = rows((8, 128))
    lane = lanes((8, 128))
    for j in range(16):
        columns[j * 8 : j * 8 + 8, :] = jnp.zeros((8, 128), F32)
    for side, received in enumerate((from_low, from_high)):
        totals = [None] * 4
        for a in STEPS:
            edge = roll(received[32:40, :], -a, 1)
            for group in range(4):
                middle = roll(received[group * 8 : group * 8 + 8, :], -a, 1)
                below = jnp.where(row == 0, edge[group : group + 1, :], roll(middle, 1, 0))
                above = jnp.where(row == 7, edge[4 + group : 5 + group, :], roll(middle, -1, 0))
                k = (a + 1) * 3
                part = (
                    face_z[side, k] * below
                    + face_z[side, k + 1] * middle
                    + face_z[side, k + 2] * above
                )
                totals[group] = part if totals[group] is None else totals[group] + part
        for group in range(4):
            for slot in range(4):
                j = group * 4 + slot
                inside = (lane >= side * 64) & (lane < side * 64 + 32)
                part = roll(totals[group], side * 64 - slot * 32, 1)
                columns[j * 8 : j * 8 + 8, :] += jnp.where(inside, part, 0.0)
    value = columns[...]
    upper = value.astype(BF16)
    lower = (value - upper.astype(F32)).astype(BF16)
    both = jnp.concatenate([upper, lower], axis=0)
    product = lax.dot_general(both, edge_basis[...], NT, preferred_element_type=F32)
    first = partial[...] + fold_rows(product[0:128] + product[128:256])
    payload[0:8, :] = pack(first) * scale
    payload[8:16, :] = gram[...]


def project(parts, given, columns, flat, image, coefficients):
    total = parts[0]
    for k in range(1, parts.shape[0]):
        total = total + parts[k]
    first = unpack(total[0:8], 2)
    gram = unpack(total[8:16], 4)
    applied = jnp.zeros((16, 256), F32)
    for i in range(32):
        applied = applied + first[:, i * 8 : i * 8 + 1] * gram[i : i + 1, :]
    both = first + (first - applied)
    pick = (lanes((32, 256)) == 8 * rows((32, 256))).astype(F32)
    coefficients[...] = lax.dot_general(
        pick, both, NT, precision=lax.Precision.HIGHEST, preferred_element_type=F32
    )
    wide = (both.reshape(16, 1, 256) * same_row()[None]).reshape(128, 256)
    upper = wide.astype(BF16)
    lower = (wide - upper.astype(F32)).astype(BF16)
    left = jnp.concatenate([upper, lower], axis=0)
    lane = lanes((128, 128))
    column = columns[...]
    for x in range(16):
        product = jnp.dot(left, flat[:, x * 128 : x * 128 + 128], preferred_element_type=F32)
        block = given[:, x].reshape(128, 128)
        block = block + jnp.where(lane == 0, roll(column, -(1 + x), 1), 0.0)
        block = block + jnp.where(lane == 127, roll(column, 62 - x, 1), 0.0)
        block = block - (product[0:128] + product[128:256])
        image[:, x] = block.reshape(16, 8, 128)


def shifted(low_out, high_out, axis):
    count = lax.axis_size(axis)
    forward = [(i, i + 1) for i in range(count - 1)]
    backward = [(target, source) for source, target in forward]
    return lax.ppermute(high_out, axis, forward), lax.ppermute(low_out, axis, backward)


def summed(values, axis, last=False):
    copies = jnp.broadcast_to(values[None], (lax.axis_size(axis),) + values.shape)
    parts = lax.all_to_all(copies, axis, 0, 0)
    return parts if last else parts.sum(0)


def local(basis, krylov, center, couplings):
    cells = krylov[0].size * lax.axis_size("gx") * lax.axis_size("gy") * lax.axis_size("gz")
    scale = 1.0 / cells
    face = like((16, 16, 128))
    low, high = call("y_faces", y_faces, (face, face), data=1 << 20)(krylov)
    y_low, y_high = shifted(low, high, "gy")
    small = like((4, 8, 128))
    image, z_high, z_low, face_x, face_y, face_z = call(
        "interior",
        interior,
        (
            like((16, 16, 8, 128)),
            small,
            small,
            like((2, 9, 8, 128)),
            like((2, 9, 16, 128)),
            like((2, 9, 8, 128)),
        ),
        scratch=[pltpu.VMEM((27, 16, 8, 128), F32), pltpu.VMEM((18, 16, 8, 128), F32)],
        flops=1 << 24,
        data=4 << 20,
    )(krylov, center, couplings)
    side = like((160, 128))
    low, high = call("x_faces", x_faces, (side, side), data=1 << 20)(krylov, y_low, y_high, z_high)
    x_low, x_high = shifted(low, high, "gx")
    flat, gram, edge_basis, edge_y = call(
        "basis",
        lambda *refs: basis_kernel(scale, *refs),
        (
            like((256, 2048), BF16),
            like((8, 128)),
            like((256, 128), BF16),
            like((2, 8, 128)),
        ),
        flops=1 << 28,
        data=2 << 20,
    )(basis, y_low, y_high)
    end = like((40, 128))
    high, low = call("z_faces", z_faces, (end, end), data=1 << 18)(z_high, z_low, edge_y, x_low, x_high)
    from_low, from_high = shifted(low, high, "gz")
    image, partial = call(
        "corrections",
        corrections,
        (like((16, 16, 8, 128)), like((16, 256))),
        scratch=[pltpu.VMEM((256, 2048), BF16)],
        flops=1 << 28,
        data=4 << 20,
    )(y_low, y_high, x_low, x_high, face_x, face_y, flat, image)
    columns, payload = call(
        "finish",
        lambda *refs: finish(scale, *refs),
        (like((128, 128)), like((16, 128))),
        data=1 << 18,
    )(from_low, from_high, face_z, edge_basis, partial, gram)
    payload = summed(payload, "gz")
    payload = summed(payload, "gx")
    parts = summed(payload, "gy", last=True)
    projected, coefficients = call(
        "project",
        project,
        (like((16, 16, 8, 128)), like((32, 16))),
        flops=1 << 28,
        data=3 << 20,
    )(parts, image, columns, flat)
    return projected, coefficients


def solution(mesh):
    in_specs = (
        P(None, "gx", "gy", "gz"),
        P(None, "gx", "gy", "gz"),
        P("gx", "gy", "gz"),
        P(None, "gx", "gy", "gz"),
    )
    out_specs = (P(None, "gx", "gy", "gz"), P())
    return jax.shard_map(local, mesh=mesh, in_specs=in_specs, out_specs=out_specs, check_vma=False)
```

time: 262 us -> 78.4 us (0.30)
  blocking collectives: 198 us -> 43 us
  local copies, waits for them, and re-layouts: 17.2 us -> 1.92 us
  other arithmetic: 13 us -> 0.02 us
  Pallas kernels: 0 us -> 10.8 us
  matrix products: 7.09 us -> 0 us
  waiting for transfers between devices: 9.25 us -> 5.42 us
    psum x2 -> x0, blocking collectives: 198 us -> none  [the longest x1 103 us: local(): first = lax.psum(local_first, ('gx', 'gy', 'gz'))]
    all_to_all x0 -> x3, blocking collectives: none -> 43 us  [summed(): parts = lax.all_to_all(copies, axis, 0, 0)]
    pallas_call x0 -> x8, Pallas kernels: none -> 10.8 us  [the longest x1 4.35 us: local(): call('interior', interior, (like((16, 16, 8, 128)), small, small, like((2...]
    add x2 -> x0, other arithmetic: 7.57 us -> none  [the longest x1 6.97 us: local(): image = image + couplings[which].astype(jnp.float32)[None] * moved]
    dot_general x4 -> x0, matrix products: 7.09 us -> none  [the longest x1 2.7 us: local(): jnp.dot(first.T, flat_basis, precision=lax.Precision.HIGHEST, preferred_e...]
    slice x5 -> x0, local copies, waits for them, and re-layouts: 7.01 us -> none  [the longest x3 4.56 us: extended(): lax.slice_in_dim(block, block.shape[dim] - width, None, axis=dim)]
    ppermute x2 -> x0, local copies, waits for them, and re-layouts: 5.1 us -> none  [the longest x1 2.56 us: extended(): lax.ppermute(lax.slice_in_dim(block, 0, width, axis=dim), axis, backward)]
    ppermute x6, waiting for transfers between devices: 9.25 us -> 5.42 us  [the longest x3 5.41 us: shifted(): lax.ppermute(low_out, axis, backward)]
  transfers between devices with their start and end apart: 6 -> 6, of which waited for: 4 -> 2; matrix products, arithmetic and copies ran while one was open for 3% -> 0% of each run, Pallas kernels for 0% -> 10%
where the time goes in v2:
time: 78.4 us; the launch traced here: 78 us
  blocking collectives  43 us (55%)
  starting transfers between devices  16 us (20%)
  Pallas kernels  10.8 us (14%)
  waiting for transfers between devices  5.42 us (7%)
  local copies, waits for them, and re-layouts  1.92 us (2%)
  between operations  0.81 us (1%)
    all_to_all x3, blocking collectives, summed(): parts = lax.all_to_all(copies, axis, 0, 0)  43 us
    ppermute x3, starting transfers between devices, shifted(): lax.ppermute(high_out, axis, forward)  9.82 us
    ppermute x3, starting transfers between devices, shifted(): lax.ppermute(low_out, axis, backward)  6.23 us
    ppermute x3, waiting for transfers between devices, shifted(): lax.ppermute(low_out, axis, backward)  5.41 us
    pallas_call x1, Pallas kernels, local(): call('interior', interior, (like((16, 16, 8, 128)), small, small, like((2...  4.35 us
    pallas_call x1, Pallas kernels, local(): call('project', project, (like((16, 16, 8, 128)), like((32, 16))), flops=...  2.2 us
    pallas_call x1, Pallas kernels, local(): call('corrections', corrections, (like((16, 16, 8, 128)), like((16, 256))...  2.16 us
  transfers between devices with their start and end apart: 6, of which 2 were waited for; matrix products, arithmetic and copies ran while one was open for 0% of the time, Pallas kernels for 10%

profile of v2, /device:TPU:2, one launch (start us, length us, event | category | flops | bytes accessed | tf_op | source)
XLA Modules:
  0.0 78.0 jit_solution(12360797112539449125)
XLA Ops:
  0.6 0.0 copy-start
  0.6 1.2 %copy-done = f32[16,16,8,128]{3,2,1,0:T(8,128)S(1)} copy-done((f32[16,16,8,128]{3,2,1,0:T(8,128)S(1)}, f32[16,16,8,128]{3,2,1,0:T(8,128)}, u32[]{:S(2)}) %copy-start) | copy-done | bytes 1048600
  1.9 0.0 copy-start.2
  1.9 0.0 copy-start.3
  1.9 0.1 y_faces.1
  2.0 3.6 %collective-permute-start = (f32[16,16,128]{2,1,0:T(8,128)S(1)}, f32[16,16,128]{2,1,0:T(8,128)S(1)}, u32[]{:S(2)}, u32[]{:S(2)}) collective-permute-start(f32[16,16,128]{2,1,0:T(8,128)S(1)} %get-tuple-element.24), channel_id=1, source_target_pairs={{0,8},{8,16},{16,24},{24,32},{32,40},{40,48},{48,56},{1,9},{9,17},... | collective-permute-start | bytes 393224 | tf_op jit(solution)/shard_map/ppermute | solution.py:358
  5.6 1.3 %collective-permute-start.1 = (f32[16,16,128]{2,1,0:T(8,128)S(1)}, f32[16,16,128]{2,1,0:T(8,128)S(1)}, u32[]{:S(2)}, u32[]{:S(2)}) collective-permute-start(f32[16,16,128]{2,1,0:T(8,128)S(1)} %get-tuple-element.25), channel_id=1, source_target_pairs={{8,0},{16,8},{24,16},{32,24},{40,32},{48,40},{56,48},{9,1},{17,9},... | collective-permute-start | bytes 393224 | tf_op jit(solution)/shard_map/ppermute | solution.py:358
  6.9 0.0 copy-done.2
  6.9 0.0 copy-done.3
  7.0 4.4 %interior.1 = (f32[16,16,8,128]{3,2,1,0:T(8,128)S(1)}, f32[4,8,128]{2,1,0:T(8,128)S(1)}, f32[4,8,128]{2,1,0:T(8,128)S(1)}, f32[2,9,8,128]{3,2,1,0:T(8,128)S(1)},...) custom-call(f32[16,16,8,128]{3,2,1,0:T(8,128)S(1)} %copy-done, bf16[16,8,128]{2,1,0:T(8,128)(2,1)S(1)} %copy-done.3, ...), custom_call_target="tpu_custom_call" | custom-call | flops 16777216 | bytes 4194304 | tf_op jit(solution)/shard_map/interior/pallas_call | solution.py:374
  11.3 0.0 copy-start.1
  11.3 0.0 collective-permute-done.refs_1_.y_low
  11.3 1.2 %collective-permute-done.1.refs_2_.y_high = f32[16,16,128]{2,1,0:T(8,128)S(1)} collective-permute-done((f32[16,16,128]{2,1,0:T(8,128)S(1)}, f32[16,16,128]{2,1,0:T(8,128)S(1)}, u32[]{:S(2)}, u32[]{:S(2)}) %collective-permute-start.1) | collective-permute-done | bytes 131104 | tf_op jit(solution)/shard_map/ppermute | solution.py:358
  12.5 4.3 %collective-permute-start.2 = (f32[160,128]{1,0:T(8,128)S(1)}, f32[160,128]{1,0:T(8,128)S(1)}, u32[]{:S(2)}, u32[]{:S(2)}) collective-permute-start(f32[160,128]{1,0:T(8,128)S(1)} %get-tuple-element.27), channel_id=1, source_target_pairs={{0,64},{64,128},{128,192},{192,256},{256,320},{320,384},{384,448},... | collective-permute-start | bytes 245768 | tf_op jit(solution)/shard_map/ppermute | solution.py:358
  16.8 1.3 %collective-permute-start.3 = (f32[160,128]{1,0:T(8,128)S(1)}, f32[160,128]{1,0:T(8,128)S(1)}, u32[]{:S(2)}, u32[]{:S(2)}) collective-permute-start(f32[160,128]{1,0:T(8,128)S(1)} %get-tuple-element.28), channel_id=1, source_target_pairs={{64,0},{128,64},{192,128},{256,192},{320,256},{384,320},{448,384},... | collective-permute-start | bytes 245768 | tf_op jit(solution)/shard_map/ppermute | solution.py:358
  18.1 0.0 copy-done.1
  18.1 1.1 %basis.1 = (bf16[256,2048]{1,0:T(8,128)(2,1)S(1)}, f32[8,128]{1,0:T(8,128)S(1)}, bf16[256,128]{1,0:T(8,128)(2,1)S(1)}, f32[2,8,128]{2,1,0:T(8,128)S(1)}) custom-call(bf16[32,16,8,128]{3,2,1,0:T(8,128)(2,1)S(1)} %copy-done.1, f32[16,16,128]{2,1,0:T(8,128)S(1)} %collective-permute-done.refs_1_.y_low, f32[16,16,128]{2,1,0:T(8,128)S(1)} %collective-permute-done.1.refs_2_.y_high), custom_call_target="tpu_custom_call" | custom-call | flops 268435456 | bytes 2097152 | tf_op jit(solution)/shard_map/basis/pallas_call | solution.py:392
  19.3 0.0 collective-permute-done.2.x_low
  19.3 4.2 %collective-permute-done.3.x_high = f32[160,128]{1,0:T(8,128)S(1)} collective-permute-done((f32[160,128]{1,0:T(8,128)S(1)}, f32[160,128]{1,0:T(8,128)S(1)}, u32[]{:S(2)}, u32[]{:S(2)}) %collective-permute-start.3) | collective-permute-done | bytes 81952 | tf_op jit(solution)/shard_map/ppermute | solution.py:358
  23.5 0.1 z_faces.1
  23.7 1.9 %collective-permute-start.4 = (f32[40,128]{1,0:T(8,128)S(1)}, f32[40,128]{1,0:T(8,128)S(1)}, u32[]{:S(2)}, u32[]{:S(2)}) collective-permute-start(f32[40,128]{1,0:T(8,128)S(1)} %get-tuple-element.29), channel_id=1, source_target_pairs={{0,1},{1,2},{2,3},{3,4},{4,5},{5,6},{6,7},{8,9},{9,10},{10,11},{11... | collective-permute-start | bytes 61448 | tf_op jit(solution)/shard_map/ppermute | solution.py:358
  25.6 3.6 %collective-permute-start.5 = (f32[40,128]{1,0:T(8,128)S(1)}, f32[40,128]{1,0:T(8,128)S(1)}, u32[]{:S(2)}, u32[]{:S(2)}) collective-permute-start(f32[40,128]{1,0:T(8,128)S(1)} %get-tuple-element.30), channel_id=1, source_target_pairs={{1,0},{2,1},{3,2},{4,3},{5,4},{6,5},{7,6},{9,8},{10,9},{11,10},{12... | collective-permute-start | bytes 61448 | tf_op jit(solution)/shard_map/ppermute | solution.py:358
  29.2 2.2 %corrections.1 = (f32[16,16,8,128]{3,2,1,0:T(8,128)S(1)}, f32[16,256]{1,0:T(8,128)S(1)}) custom-call(f32[16,16,128]{2,1,0:T(8,128)S(1)} %collective-permute-done.refs_1_.y_low, f32[16,16,128]{2,1,0:T(8,128)S(1)} %collective-permute-done.1.refs_2_.y_high, f32[160,128]{1,0:T(8,128)S(1)} %collective-permute-done.2.x_low, ...), custom_call_target="tpu_custom_call" | custom-call | flops 268435456 | bytes 4194304 | tf_op jit(solution)/shard_map/corrections/pallas_call | solution.py:407
  31.4 0.0 collective-permute-done.4.refs_0_
  31.4 0.0 collective-permute-done.5.refs_1_
  31.4 0.6 finish.1
  32.0 9.0 %all_to_all.15 = f32[8,16,128]{2,1,0:T(8,128)S(1)} all-to-all(f32[8,16,128]{2,1,0:T(8,128)S(1)} %broadcast_in_dim.6), channel_id=1, replica_groups=mesh['gx'=8,'gy'=8,'gz'=8] {'gz'}, dimensions={0} | all-to-all | bytes 131072 | tf_op jit(solution)/shard_map/all_to_all | solution.py:363
  41.0 17.5 %all_to_all.16 = f32[8,16,128]{2,1,0:T(8,128)S(1)} all-to-all(f32[8,16,128]{2,1,0:T(8,128)S(1)} %broadcast_in_dim.7), channel_id=1, replica_groups=mesh['gx'=8,'gy'=8,'gz'=8] {'gx'}, dimensions={0} | all-to-all | bytes 131072 | tf_op jit(solution)/shard_map/all_to_all | solution.py:363
  58.6 16.5 %all_to_all.17.parts = f32[8,16,128]{2,1,0:T(8,128)S(1)} all-to-all(f32[8,16,128]{2,1,0:T(8,128)S(1)} %broadcast_in_dim.8), channel_id=1, replica_groups=mesh['gx'=8,'gy'=8,'gz'=8] {'gy'}, dimensions={0} | all-to-all | bytes 131072 | tf_op jit(solution)/shard_map/all_to_all | solution.py:363
  75.1 2.2 %project.1 = (f32[16,16,8,128]{3,2,1,0:T(8,128)}, f32[32,16]{1,0:T(8,128)S(1)}) custom-call(f32[8,16,128]{2,1,0:T(8,128)S(1)} %all_to_all.17.parts, f32[16,16,8,128]{3,2,1,0:T(8,128)S(1)} %get-tuple-element.40.given, f32[128,128]{1,0:T(8,128)S(1)} %get-tuple-element.41.columns, bf16[256,2048]{1,0:T(8,128)(2,1)S(1)} %get-tuple-element.35.flat), custom_call_target="tpu_custom_call" | custom-call | flops 268435456 | bytes 3145728 | tf_op jit(solution)/shard_map/project/pallas_call | solution.py:424
  77.3 0.7 copy.7
  (6 shorter events, 0.1 us)
Async XLA Ops:
  0.6 1.2 %copy-start = (f32[16,16,8,128]{3,2,1,0:T(8,128)S(1)}, f32[16,16,8,128]{3,2,1,0:T(8,128)}, u32[]{:S(2)}) copy-start(f32[16,16,8,128]{3,2,1,0:T(8,128)} %krylov.5) | copy-start | bytes 3145732
  1.9 5.1 %copy-start.2 = (bf16[26,16,8,128]{3,2,1,0:T(8,128)(2,1)S(1)}, bf16[26,16,8,128]{3,2,1,0:T(8,128)(2,1)}, u32[]{:S(2)}) copy-start(bf16[26,16,8,128]{3,2,1,0:T(8,128)(2,1)} %couplings.1) | copy-start | bytes 2555908
  1.9 5.1 %copy-start.3 = (bf16[16,8,128]{2,1,0:T(8,128)(2,1)S(1)}, bf16[16,8,128]{2,1,0:T(8,128)(2,1)}, u32[]{:S(2)}) copy-start(bf16[16,8,128]{2,1,0:T(8,128)(2,1)} %center.1) | copy-start | bytes 98308
  2.0 9.3 %collective-permute-start = (f32[16,16,128]{2,1,0:T(8,128)S(1)}, f32[16,16,128]{2,1,0:T(8,128)S(1)}, u32[]{:S(2)}, u32[]{:S(2)}) collective-permute-start(f32[16,16,128]{2,1,0:T(8,128)S(1)} %get-tuple-element.24), channel_id=1, source_target_pairs={{0,8},{8,16},{16,24},{24,32},{32,40},{40,48},{48,56},{1,9},{9,17},... | collective-permute-start | bytes 393224 | tf_op jit(solution)/shard_map/ppermute | solution.py:358
  5.6 6.9 %collective-permute-start.1 = (f32[16,16,128]{2,1,0:T(8,128)S(1)}, f32[16,16,128]{2,1,0:T(8,128)S(1)}, u32[]{:S(2)}, u32[]{:S(2)}) collective-permute-start(f32[16,16,128]{2,1,0:T(8,128)S(1)} %get-tuple-element.25), channel_id=1, source_target_pairs={{8,0},{16,8},{24,16},{32,24},{40,32},{48,40},{56,48},{9,1},{17,9},... | collective-permute-start | bytes 393224 | tf_op jit(solution)/shard_map/ppermute | solution.py:358
  11.3 6.8 %copy-start.1 = (bf16[32,16,8,128]{3,2,1,0:T(8,128)(2,1)S(1)}, bf16[32,16,8,128]{3,2,1,0:T(8,128)(2,1)}, u32[]{:S(2)}) copy-start(bf16[32,16,8,128]{3,2,1,0:T(8,128)(2,1)} %refs_0_.1) | copy-start | bytes 3145732
  12.5 6.7 %collective-permute-start.2 = (f32[160,128]{1,0:T(8,128)S(1)}, f32[160,128]{1,0:T(8,128)S(1)}, u32[]{:S(2)}, u32[]{:S(2)}) collective-permute-start(f32[160,128]{1,0:T(8,128)S(1)} %get-tuple-element.27), channel_id=1, source_target_pairs={{0,64},{64,128},{128,192},{192,256},{256,320},{320,384},{384,448},... | collective-permute-start | bytes 245768 | tf_op jit(solution)/shard_map/ppermute | solution.py:358
  16.8 6.7 %collective-permute-start.3 = (f32[160,128]{1,0:T(8,128)S(1)}, f32[160,128]{1,0:T(8,128)S(1)}, u32[]{:S(2)}, u32[]{:S(2)}) collective-permute-start(f32[160,128]{1,0:T(8,128)S(1)} %get-tuple-element.28), channel_id=1, source_target_pairs={{64,0},{128,64},{192,128},{256,192},{320,256},{384,320},{448,384},... | collective-permute-start | bytes 245768 | tf_op jit(solution)/shard_map/ppermute | solution.py:358
  23.7 7.7 %collective-permute-start.4 = (f32[40,128]{1,0:T(8,128)S(1)}, f32[40,128]{1,0:T(8,128)S(1)}, u32[]{:S(2)}, u32[]{:S(2)}) collective-permute-start(f32[40,128]{1,0:T(8,128)S(1)} %get-tuple-element.29), channel_id=1, source_target_pairs={{0,1},{1,2},{2,3},{3,4},{4,5},{5,6},{6,7},{8,9},{9,10},{10,11},{11... | collective-permute-start | bytes 61448 | tf_op jit(solution)/shard_map/ppermute | solution.py:358
  25.6 5.8 %collective-permute-start.5 = (f32[40,128]{1,0:T(8,128)S(1)}, f32[40,128]{1,0:T(8,128)S(1)}, u32[]{:S(2)}, u32[]{:S(2)}) collective-permute-start(f32[40,128]{1,0:T(8,128)S(1)} %get-tuple-element.30), channel_id=1, source_target_pairs={{1,0},{2,1},{3,2},{4,3},{5,4},{6,5},{7,6},{9,8},{10,9},{11,10},{12... | collective-permute-start | bytes 61448 | tf_op jit(solution)/shard_map/ppermute | solution.py:358

commit v3 on v2

--- a/solution.py
+++ b/solution.py
@@ -12,7 +12,7 @@
 STEPS = (-1, 0, 1)
 
 
-def call(name, body, out, scratch=(), flops=0, data=0, aliases=None):
+def call(name, body, out, scratch=(), flops=0, data=0, specs=None):
     single = not isinstance(out, (tuple, list))
     shapes = (out,) if single else tuple(out)
     built = pl.pallas_call(
@@ -20,8 +20,8 @@
         name=name,
         out_shape=shapes[0] if single else shapes,
         scratch_shapes=list(scratch),
-        input_output_aliases=aliases or {},
-        compiler_params=pltpu.CompilerParams(vmem_limit_bytes=40 << 20),
+        **(specs or {}),
+        compiler_params=pltpu.CompilerParams(vmem_limit_bytes=16 << 20),
         cost_estimate=pl.CostEstimate(flops=flops, bytes_accessed=data, transcendentals=0),
     )
     return built
@@ -54,9 +54,15 @@
     return total
 
 
-def y_faces(krylov, low, high):
-    low[...] = krylov[:, :, 0, :]
-    high[...] = krylov[:, :, 7, :]
+def y_faces(krylov, low, high, done):
+    copies = [
+        pltpu.make_async_copy(krylov.at[:, :, y, :], out, done.at[k])
+        for k, (out, y) in enumerate(((low, 0), (high, 7)))
+    ]
+    for copy in copies:
+        copy.start()
+    for copy in copies:
+        copy.wait()
 
 
 def number(a, b, c):
@@ -232,9 +238,10 @@
         edge_y[side] = total
 
 
-def z_faces(z_high, z_low, edge_y, x_low, x_high, out_high, out_low):
+def z_faces(odd, z_high, z_low, edge_y, x_low, x_high, near, far):
     lane = lanes((8, 128))
-    for side, (own, out) in enumerate(((z_high, out_high), (z_low, out_low))):
+    values = []
+    for side, own in enumerate((z_high, z_low)):
         for group in range(5):
             value = edge_y[side] if group == 4 else own[group]
             for slot in range(4):
@@ -243,7 +250,12 @@
                     place = slot * 32 + q
                     part = roll(face[first : first + 8, :], place + 1 - side, 1)
                     value = jnp.where(lane == place, part, value)
-            out[group * 8 : group * 8 + 8, :] = value
+            values.append(value)
+    flipped = odd[0] == 1
+    for group in range(5):
+        high, low = values[group], values[5 + group]
+        near[group * 8 : group * 8 + 8, :] = jnp.where(flipped, low, high)
+        far[group * 8 : group * 8 + 8, :] = jnp.where(flipped, high, low)
 
 
 def corrections(y_low, y_high, x_low, x_high, face_x, face_y, flat, given, image, partial, halves):
@@ -286,12 +298,15 @@
     partial[...] = fold_rows(product[0:128] + product[128:256])
 
 
-def finish(scale, from_low, from_high, face_z, edge_basis, partial, gram, columns, payload):
+def finish(scale, odd, near, far, face_z, edge_basis, partial, gram, columns, payload):
     row = rows((8, 128))
     lane = lanes((8, 128))
     for j in range(16):
         columns[j * 8 : j * 8 + 8, :] = jnp.zeros((8, 128), F32)
-    for side, received in enumerate((from_low, from_high)):
+    flipped = odd[0] == 1
+    for side in range(2):
+        pair = (far, near) if side == 0 else (near, far)
+        received = jnp.where(flipped, pair[1][...], pair[0][...])
         totals = [None] * 4
         for a in STEPS:
             edge = roll(received[32:40, :], -a, 1)
@@ -322,7 +337,7 @@
     payload[8:16, :] = gram[...]
 
 
-def project(parts, given, columns, flat, image, coefficients):
+def project(parts, given, columns, flat, image, coefficients, ready, done):
     total = parts[0]
     for k in range(1, parts.shape[0]):
         total = total + parts[k]
@@ -334,7 +349,7 @@
     both = first + (first - applied)
     pick = (lanes((32, 256)) == 8 * rows((32, 256))).astype(F32)
     coefficients[...] = lax.dot_general(
-        pick, both, NT, precision=lax.Precision.HIGHEST, preferred_element_type=F32
+        both, pick, NT, precision=lax.Precision.HIGHEST, preferred_element_type=F32
     )
     wide = (both.reshape(16, 1, 256) * same_row()[None]).reshape(128, 256)
     upper = wide.astype(BF16)
@@ -342,13 +357,24 @@
     left = jnp.concatenate([upper, lower], axis=0)
     lane = lanes((128, 128))
     column = columns[...]
-    for x in range(16):
-        product = jnp.dot(left, flat[:, x * 128 : x * 128 + 128], preferred_element_type=F32)
-        block = given[:, x].reshape(128, 128)
-        block = block + jnp.where(lane == 0, roll(column, -(1 + x), 1), 0.0)
-        block = block + jnp.where(lane == 127, roll(column, 62 - x, 1), 0.0)
-        block = block - (product[0:128] + product[128:256])
-        image[:, x] = block.reshape(16, 8, 128)
+    above = roll(column, -65, 1)
+    mixed = [jnp.where(lane % 2 == 1 - k, column, above) for k in range(2)]
+    ends = (lane == 0) | (lane == 127)
+    copies = []
+    for pair in range(8):
+        product = jnp.dot(left, flat[:, pair * 256 : pair * 256 + 256], preferred_element_type=F32)
+        product = product[0:128] + product[128:256]
+        for inner in range(2):
+            x = pair * 2 + inner
+            block = given[:, x].reshape(128, 128)
+            block = block + jnp.where(ends, roll(mixed[x % 2], -(1 + x), 1), 0.0)
+            block = block - product[:, inner * 128 : inner * 128 + 128]
+            ready[:, x] = block.reshape(16, 8, 128)
+        span = pl.ds(pair * 2, 2)
+        copies.append(pltpu.make_async_copy(ready.at[:, span], image.at[:, span], done.at[pair]))
+        copies[-1].start()
+    for copy in copies:
+        copy.wait()
 
 
 def shifted(low_out, high_out, axis):
@@ -368,7 +394,14 @@
     cells = krylov[0].size * lax.axis_size("gx") * lax.axis_size("gy") * lax.axis_size("gz")
     scale = 1.0 / cells
     face = like((16, 16, 128))
-    low, high = call("y_faces", y_faces, (face, face), data=1 << 20)(krylov)
+    low, high = call(
+        "y_faces",
+        y_faces,
+        (face, face),
+        scratch=[pltpu.SemaphoreType.DMA((2,))],
+        data=1 << 18,
+        specs={"in_specs": [pl.BlockSpec(memory_space=pltpu.HBM)]},
+    )(pltpu.with_memory_space_constraint(krylov, pltpu.HBM))
     y_low, y_high = shifted(low, high, "gy")
     small = like((4, 8, 128))
     image, z_high, z_low, face_x, face_y, face_z = call(
@@ -402,8 +435,16 @@
         data=2 << 20,
     )(basis, y_low, y_high)
     end = like((40, 128))
-    high, low = call("z_faces", z_faces, (end, end), data=1 << 18)(z_high, z_low, edge_y, x_low, x_high)
-    from_low, from_high = shifted(low, high, "gz")
+    odd = jnp.bitwise_and(lax.axis_index("gz"), 1).astype(jnp.int32).reshape(1)
+    scalar = pl.BlockSpec(memory_space=pltpu.SMEM)
+    block = pl.BlockSpec()
+    near, far = call(
+        "z_faces", z_faces, (end, end), data=1 << 18, specs={"in_specs": [scalar] + [block] * 5}
+    )(odd, z_high, z_low, edge_y, x_low, x_high)
+    count = lax.axis_size("gz")
+    near = lax.ppermute(near, "gz", [(i, i ^ 1) for i in range(count)])
+    inner = range(1, count - 1)
+    far = lax.ppermute(far, "gz", [(i, ((i + 1) ^ 1) - 1) for i in inner])
     image, partial = call(
         "corrections",
         corrections,
@@ -417,18 +458,26 @@
         lambda *refs: finish(scale, *refs),
         (like((128, 128)), like((16, 128))),
         data=1 << 18,
-    )(from_low, from_high, face_z, edge_basis, partial, gram)
+        specs={"in_specs": [scalar] + [block] * 6},
+    )(odd, near, far, face_z, edge_basis, partial, gram)
     payload = summed(payload, "gz")
     payload = summed(payload, "gx")
     parts = summed(payload, "gy", last=True)
     projected, coefficients = call(
         "project",
         project,
-        (like((16, 16, 8, 128)), like((32, 16))),
+        (like((16, 16, 8, 128)), like((16, 32))),
+        scratch=[pltpu.VMEM((16, 16, 8, 128), F32), pltpu.SemaphoreType.DMA((8,))],
         flops=1 << 28,
         data=3 << 20,
+        specs={
+            "out_specs": (
+                pl.BlockSpec(memory_space=pl.ANY),
+                pl.BlockSpec(memory_space=pltpu.VMEM),
+            )
+        },
     )(parts, image, columns, flat)
-    return projected, coefficients
+    return projected, coefficients.T
 
 
 def solution(mesh):

time: 78.4 us -> 81.3 us (1.037)
  Pallas kernels: 10.8 us -> 14.3 us
  starting transfers between devices: 16 us -> 14.8 us
  blocking collectives: 43 us -> 44.1 us
  waiting for transfers between devices: 5.42 us -> 4.59 us
    ppermute x0 -> x2, starting transfers between devices: none -> 4.47 us  [the longest x1 2.55 us: local(): far = lax.ppermute(far, 'gz', [(i, (i + 1 ^ 1) - 1) for i in inner])]
    ppermute x3 -> x2, starting transfers between devices: 6.23 us -> 2.58 us  [shifted(): lax.ppermute(low_out, axis, backward)]
    ppermute x3 -> x2, starting transfers between devices: 9.82 us -> 7.77 us  [shifted(): lax.ppermute(high_out, axis, forward)]
    pallas_call x3, Pallas kernels: 2.48 us -> 4.47 us  [the longest x1 2.34 us: local(): call('project', project, (like((16, 16, 8, 128)), like((16, 32))), scratc...]
    all_to_all x3, blocking collectives: 43 us -> 44.1 us  [summed(): parts = lax.all_to_all(copies, axis, 0, 0)]
    pallas_call x1, Pallas kernels: 2.16 us -> 3.11 us  [local(): call('corrections', corrections, (like((16, 16, 8, 128)), like((16, 256))...]
    ppermute x3 -> x2, waiting for transfers between devices: 5.41 us -> 4.58 us  [shifted(): lax.ppermute(low_out, axis, backward)]
    unnamed x8 -> x20, local copies, waits for them, and re-layouts: 1.23 us -> 1.95 us
  transfers between devices with their start and end apart: 6 -> 6, of which waited for: 2 -> 1; matrix products, arithmetic and copies ran while one was open for 0% -> 0% of each run, Pallas kernels for 10% -> 11%
where the time goes in v3:
time: 81.3 us; the launch traced here: 80.7 us
  blocking collectives  44.1 us (54%)
  starting transfers between devices  14.8 us (18%)
  Pallas kernels  14.3 us (18%)
  waiting for transfers between devices  4.59 us (6%)
  local copies, waits for them, and re-layouts  1.97 us (2%)
  between operations  0.89 us (1%)
    all_to_all x3, blocking collectives, summed(): parts = lax.all_to_all(copies, axis, 0, 0)  44.1 us
    ppermute x2, starting transfers between devices, shifted(): lax.ppermute(high_out, axis, forward)  7.77 us
    ppermute x2, waiting for transfers between devices, shifted(): lax.ppermute(low_out, axis, backward)  4.58 us
    pallas_call x1, Pallas kernels, local(): call('interior', interior, (like((16, 16, 8, 128)), small, small, like((2...  4.35 us
    pallas_call x1, Pallas kernels, local(): call('corrections', corrections, (like((16, 16, 8, 128)), like((16, 256))...  3.11 us
    ppermute x2, starting transfers between devices, shifted(): lax.ppermute(low_out, axis, backward)  2.58 us
    ppermute x1, starting transfers between devices, local(): far = lax.ppermute(far, 'gz', [(i, (i + 1 ^ 1) - 1) for i in inner])  2.55 us
    pallas_call x1, Pallas kernels, local(): call('project', project, (like((16, 16, 8, 128)), like((16, 32))), scratc...  2.34 us
  transfers between devices with their start and end apart: 6, of which 1 were waited for; matrix products, arithmetic and copies ran while one was open for 0% of the time, Pallas kernels for 11%

profile of v3, /device:TPU:2, one launch (start us, length us, event | category | flops | bytes accessed | tf_op | source)
XLA Modules:
  0.0 80.7 jit_solution(5580347493562344911)
XLA Ops:
  0.6 0.0 copy-start
  0.6 1.1 %y_faces.1 = (f32[16,16,128]{2,1,0:T(8,128)S(1)}, f32[16,16,128]{2,1,0:T(8,128)S(1)}) custom-call(f32[16,16,8,128]{3,2,1,0:T(8,128)} %krylov.5), custom_call_target="tpu_custom_call" | custom-call | bytes 262144 | tf_op jit(solution)/shard_map/y_faces/pallas_call | solution.py:397
  1.7 3.5 %collective-permute-start = (f32[16,16,128]{2,1,0:T(8,128)S(1)}, f32[16,16,128]{2,1,0:T(8,128)S(1)}, u32[]{:S(2)}, u32[]{:S(2)}) collective-permute-start(f32[16,16,128]{2,1,0:T(8,128)S(1)} %get-tuple-element.26), channel_id=1, source_target_pairs={{0,8},{8,16},{16,24},{24,32},{32,40},{40,48},{48,56},{1,9},{9,17},... | collective-permute-start | bytes 393224 | tf_op jit(solution)/shard_map/ppermute | solution.py:384
  5.2 1.3 %collective-permute-start.1 = (f32[16,16,128]{2,1,0:T(8,128)S(1)}, f32[16,16,128]{2,1,0:T(8,128)S(1)}, u32[]{:S(2)}, u32[]{:S(2)}) collective-permute-start(f32[16,16,128]{2,1,0:T(8,128)S(1)} %get-tuple-element.27), channel_id=1, source_target_pairs={{8,0},{16,8},{24,16},{32,24},{40,32},{48,40},{56,48},{9,1},{17,9},... | collective-permute-start | bytes 393224 | tf_op jit(solution)/shard_map/ppermute | solution.py:384
  6.5 0.0 copy-done
  6.5 0.0 copy-start.2
  6.5 1.1 %copy-done.2 = bf16[26,16,8,128]{3,2,1,0:T(8,128)(2,1)S(1)} copy-done((bf16[26,16,8,128]{3,2,1,0:T(8,128)(2,1)S(1)}, bf16[26,16,8,128]{3,2,1,0:T(8,128)(2,1)}, u32[]{:S(2)}) %copy-start.2) | copy-done | bytes 851992
  7.7 0.0 copy-start.9
  7.7 0.8 copy-done.9
  8.4 4.3 %interior.1 = (f32[16,16,8,128]{3,2,1,0:T(8,128)S(1)}, f32[4,8,128]{2,1,0:T(8,128)S(1)}, f32[4,8,128]{2,1,0:T(8,128)S(1)}, f32[2,9,8,128]{3,2,1,0:T(8,128)S(1)},...) custom-call(f32[16,16,8,128]{3,2,1,0:T(8,128)S(1)} %copy-done, bf16[16,8,128]{2,1,0:T(8,128)(2,1)S(1)} %copy-done.9, ...), custom_call_target="tpu_custom_call" | custom-call | flops 16777216 | bytes 4194304 | tf_op jit(solution)/shard_map/interior/pallas_call | solution.py:407
  12.8 0.0 copy-start.3
  12.8 0.0 copy-start.5
  12.8 0.0 copy-start.7
  12.8 0.0 copy-start.1
  12.8 0.0 collective-permute-done.refs_1_.y_low
  12.9 0.0 collective-permute-done.1.refs_2_.y_high
  12.9 0.7 x_faces.1
  13.5 0.0 copy-done.3
  13.5 0.0 copy-done.5
  13.6 0.0 copy-done.7
  13.6 4.3 %collective-permute-start.2 = (f32[160,128]{1,0:T(8,128)}, f32[160,128]{1,0:T(8,128)S(1)}, u32[]{:S(2)}, u32[]{:S(2)}) collective-permute-start(f32[160,128]{1,0:T(8,128)} %get-tuple-element.29), channel_id=1, source_target_pairs={{0,64},{64,128},{128,192},{192,256},{256,320},{320,384},{384,448},... | collective-permute-start | bytes 245768 | tf_op jit(solution)/shard_map/ppermute | solution.py:384
  17.8 1.3 %collective-permute-start.3 = (f32[160,128]{1,0:T(8,128)}, f32[160,128]{1,0:T(8,128)}, u32[]{:S(2)}, u32[]{:S(2)}) collective-permute-start(f32[160,128]{1,0:T(8,128)} %get-tuple-element.30), channel_id=1, source_target_pairs={{64,0},{128,64},{192,128},{256,192},{320,256},{384,320},{448,384},... | collective-permute-start | bytes 245768 | tf_op jit(solution)/shard_map/ppermute | solution.py:384
  19.1 0.0 copy-done.1
  19.2 1.1 %basis.1 = (bf16[256,2048]{1,0:T(8,128)(2,1)S(1)}, f32[8,128]{1,0:T(8,128)S(1)}, bf16[256,128]{1,0:T(8,128)(2,1)S(1)}, f32[2,8,128]{2,1,0:T(8,128)S(1)}) custom-call(bf16[32,16,8,128]{3,2,1,0:T(8,128)(2,1)S(1)} %copy-done.1, f32[16,16,128]{2,1,0:T(8,128)S(1)} %collective-permute-done.refs_1_.y_low, f32[16,16,128]{2,1,0:T(8,128)S(1)} %collective-permute-done.1.refs_2_.y_high), custom_call_target="tpu_custom_call" | custom-call | flops 268435456 | bytes 2097152 | tf_op jit(solution)/shard_map/basis/pallas_call | solution.py:425
  20.3 0.0 copy-start.4
  20.3 0.0 collective-permute-done.2.x_low
  20.3 4.6 %collective-permute-done.3.x_high = f32[160,128]{1,0:T(8,128)} collective-permute-done((f32[160,128]{1,0:T(8,128)}, f32[160,128]{1,0:T(8,128)}, u32[]{:S(2)}, u32[]{:S(2)}) %collective-permute-start.3) | collective-permute-done | bytes 81952 | tf_op jit(solution)/shard_map/ppermute | solution.py:384
  24.9 0.0 copy-start.6
  24.9 1.1 %z_faces.1 = (f32[40,128]{1,0:T(8,128)S(1)}, f32[40,128]{1,0:T(8,128)S(1)}) custom-call(s32[1]{0:T(128)} %bitcast.odd.refs_0_, f32[4,8,128]{2,1,0:T(8,128)S(1)} %get-tuple-element.24.after.z_high, f32[4,8,128]{2,1,0:T(8,128)S(1)} %get-tuple-element.25.z_low, f32[2,8,128]{2,1,0:T(8,128)S(1)} %get-tuple-element.28.edge_y, ...), custom_call_target="tpu_custom_call" | custom-call | bytes 262144 | tf_op jit(solution)/shard_map/z_faces/pallas_call | solution.py:441
  25.9 1.9 %collective-permute-start.4 = (f32[40,128]{1,0:T(8,128)S(1)}, f32[40,128]{1,0:T(8,128)S(1)}, u32[]{:S(2)}, u32[]{:S(2)}) collective-permute-start(f32[40,128]{1,0:T(8,128)S(1)} %get-tuple-element.31), channel_id=1, source_target_pairs={{0,1},{1,0},{2,3},{3,2},{4,5},{5,4},{6,7},{7,6},{8,9},{9,8},{10,11... | collective-permute-start | bytes 61448 | tf_op jit(solution)/shard_map/ppermute | solution.py:445
  27.8 2.5 %collective-permute-start.5 = (f32[40,128]{1,0:T(8,128)S(1)}, f32[40,128]{1,0:T(8,128)S(1)}, u32[]{:S(2)}, u32[]{:S(2)}) collective-permute-start(f32[40,128]{1,0:T(8,128)S(1)} %get-tuple-element.32), channel_id=1, source_target_pairs={{1,2},{2,1},{3,4},{4,3},{5,6},{6,5},{9,10},{10,9},{11,12},{12,11},... | collective-permute-start | bytes 61448 | tf_op jit(solution)/shard_map/ppermute | solution.py:447
  30.4 0.0 copy-done.4
  30.4 0.0 copy-done.6
  30.4 0.0 copy-start.8
  30.4 3.1 %corrections.1 = (f32[16,16,8,128]{3,2,1,0:T(8,128)S(1)}, f32[16,256]{1,0:T(8,128)S(1)}) custom-call(f32[16,16,128]{2,1,0:T(8,128)S(1)} %collective-permute-done.refs_1_.y_low, f32[16,16,128]{2,1,0:T(8,128)S(1)} %collective-permute-done.1.refs_2_.y_high, f32[160,128]{1,0:T(8,128)S(1)} %collective-permute-done.2.x_low, ...), custom_call_target="tpu_custom_call" | custom-call | flops 268435456 | bytes 4194304 | tf_op jit(solution)/shard_map/corrections/pallas_call | solution.py:448
  33.6 0.0 collective-permute-done.4.refs_1_
  33.6 0.0 collective-permute-done.5.refs_2_
  33.6 0.0 copy-done.8
  33.6 0.6 finish.1
  34.2 9.1 %all_to_all.15 = f32[8,16,128]{2,1,0:T(8,128)S(1)} all-to-all(f32[8,16,128]{2,1,0:T(8,128)S(1)} %broadcast_in_dim.6), channel_id=1, replica_groups=mesh['gx'=8,'gy'=8,'gz'=8] {'gz'}, dimensions={0} | all-to-all | bytes 131072 | tf_op jit(solution)/shard_map/all_to_all | solution.py:389
  43.3 17.5 %all_to_all.16 = f32[8,16,128]{2,1,0:T(8,128)S(1)} all-to-all(f32[8,16,128]{2,1,0:T(8,128)S(1)} %broadcast_in_dim.7), channel_id=1, replica_groups=mesh['gx'=8,'gy'=8,'gz'=8] {'gx'}, dimensions={0} | all-to-all | bytes 131072 | tf_op jit(solution)/shard_map/all_to_all | solution.py:389
  60.8 17.5 %all_to_all.17.parts = f32[8,16,128]{2,1,0:T(8,128)S(1)} all-to-all(f32[8,16,128]{2,1,0:T(8,128)S(1)} %broadcast_in_dim.8), channel_id=1, replica_groups=mesh['gx'=8,'gy'=8,'gz'=8] {'gy'}, dimensions={0} | all-to-all | bytes 131072 | tf_op jit(solution)/shard_map/all_to_all | solution.py:389
  78.4 2.3 %project.1 = (f32[16,16,8,128]{3,2,1,0:T(8,128)}, f32[16,32]{1,0:T(8,128)}) custom-call(f32[8,16,128]{2,1,0:T(8,128)S(1)} %all_to_all.17.parts, f32[16,16,8,128]{3,2,1,0:T(8,128)S(1)} %get-tuple-element.42.given, f32[128,128]{1,0:T(8,128)S(1)} %get-tuple-element.43.columns, bf16[256,2048]{1,0:T(8,128)(2,1)S(1)} %get-tuple-element.37.flat), custom_call_target="tpu_custom_call" | custom-call | flops 268435456 | bytes 3145728 | tf_op jit(solution)/shard_map/project/pallas_call | solution.py:466
  (5 shorter events, 0.0 us)
Async XLA Ops:
  0.6 5.9 %copy-start = (f32[16,16,8,128]{3,2,1,0:T(8,128)S(1)}, f32[16,16,8,128]{3,2,1,0:T(8,128)}, u32[]{:S(2)}) copy-start(f32[16,16,8,128]{3,2,1,0:T(8,128)} %krylov.5) | copy-start | bytes 3145732
  1.7 11.1 %collective-permute-start = (f32[16,16,128]{2,1,0:T(8,128)S(1)}, f32[16,16,128]{2,1,0:T(8,128)S(1)}, u32[]{:S(2)}, u32[]{:S(2)}) collective-permute-start(f32[16,16,128]{2,1,0:T(8,128)S(1)} %get-tuple-element.26), channel_id=1, source_target_pairs={{0,8},{8,16},{16,24},{24,32},{32,40},{40,48},{48,56},{1,9},{9,17},... | collective-permute-start | bytes 393224 | tf_op jit(solution)/shard_map/ppermute | solution.py:384
  5.2 7.6 %collective-permute-start.1 = (f32[16,16,128]{2,1,0:T(8,128)S(1)}, f32[16,16,128]{2,1,0:T(8,128)S(1)}, u32[]{:S(2)}, u32[]{:S(2)}) collective-permute-start(f32[16,16,128]{2,1,0:T(8,128)S(1)} %get-tuple-element.27), channel_id=1, source_target_pairs={{8,0},{16,8},{24,16},{32,24},{40,32},{48,40},{56,48},{9,1},{17,9},... | collective-permute-start | bytes 393224 | tf_op jit(solution)/shard_map/ppermute | solution.py:384
  6.5 1.2 %copy-start.2 = (bf16[26,16,8,128]{3,2,1,0:T(8,128)(2,1)S(1)}, bf16[26,16,8,128]{3,2,1,0:T(8,128)(2,1)}, u32[]{:S(2)}) copy-start(bf16[26,16,8,128]{3,2,1,0:T(8,128)(2,1)} %couplings.1) | copy-start | bytes 2555908
  7.7 0.8 copy-start.9
  12.8 0.8 copy-start.3
  12.8 0.7 copy-start.5
  12.8 0.7 copy-start.7
  12.8 6.3 %copy-start.1 = (bf16[32,16,8,128]{3,2,1,0:T(8,128)(2,1)S(1)}, bf16[32,16,8,128]{3,2,1,0:T(8,128)(2,1)}, u32[]{:S(2)}) copy-start(bf16[32,16,8,128]{3,2,1,0:T(8,128)(2,1)} %refs_0_.1) | copy-start | bytes 3145732
  13.6 6.7 %collective-permute-start.2 = (f32[160,128]{1,0:T(8,128)}, f32[160,128]{1,0:T(8,128)S(1)}, u32[]{:S(2)}, u32[]{:S(2)}) collective-permute-start(f32[160,128]{1,0:T(8,128)} %get-tuple-element.29), channel_id=1, source_target_pairs={{0,64},{64,128},{128,192},{192,256},{256,320},{320,384},{384,448},... | collective-permute-start | bytes 245768 | tf_op jit(solution)/shard_map/ppermute | solution.py:384
  17.8 7.0 %collective-permute-start.3 = (f32[160,128]{1,0:T(8,128)}, f32[160,128]{1,0:T(8,128)}, u32[]{:S(2)}, u32[]{:S(2)}) collective-permute-start(f32[160,128]{1,0:T(8,128)} %get-tuple-element.30), channel_id=1, source_target_pairs={{64,0},{128,64},{192,128},{256,192},{320,256},{384,320},{448,384},... | collective-permute-start | bytes 245768 | tf_op jit(solution)/shard_map/ppermute | solution.py:384
  20.3 10.2 %copy-start.4 = (f32[2,9,16,128]{3,2,1,0:T(8,128)S(1)}, f32[2,9,16,128]{3,2,1,0:T(8,128)}, u32[]{:S(2)}) copy-start(f32[2,9,16,128]{3,2,1,0:T(8,128)} %copy-done.3) | copy-start | bytes 442372
  24.9 5.6 %copy-start.6 = (f32[2,9,8,128]{3,2,1,0:T(8,128)S(1)}, f32[2,9,8,128]{3,2,1,0:T(8,128)}, u32[]{:S(2)}) copy-start(f32[2,9,8,128]{3,2,1,0:T(8,128)} %copy-done.5) | copy-start | bytes 221188
  25.9 7.6 %collective-permute-start.4 = (f32[40,128]{1,0:T(8,128)S(1)}, f32[40,128]{1,0:T(8,128)S(1)}, u32[]{:S(2)}, u32[]{:S(2)}) collective-permute-start(f32[40,128]{1,0:T(8,128)S(1)} %get-tuple-element.31), channel_id=1, source_target_pairs={{0,1},{1,0},{2,3},{3,2},{4,5},{5,4},{6,7},{7,6},{8,9},{9,8},{10,11... | collective-permute-start | bytes 61448 | tf_op jit(solution)/shard_map/ppermute | solution.py:445
  27.8 5.7 %collective-permute-start.5 = (f32[40,128]{1,0:T(8,128)S(1)}, f32[40,128]{1,0:T(8,128)S(1)}, u32[]{:S(2)}, u32[]{:S(2)}) collective-permute-start(f32[40,128]{1,0:T(8,128)S(1)} %get-tuple-element.32), channel_id=1, source_target_pairs={{1,2},{2,1},{3,4},{4,3},{5,6},{6,5},{9,10},{10,9},{11,12},{12,11},... | collective-permute-start | bytes 61448 | tf_op jit(solution)/shard_map/ppermute | solution.py:447
  30.4 3.2 %copy-start.8 = (f32[2,9,8,128]{3,2,1,0:T(8,128)S(1)}, f32[2,9,8,128]{3,2,1,0:T(8,128)}, u32[]{:S(2)}) copy-start(f32[2,9,8,128]{3,2,1,0:T(8,128)} %copy-done.7) | copy-start | bytes 221188

commit v4 on v3

--- a/solution.py
+++ b/solution.py
@@ -21,7 +21,7 @@
         out_shape=shapes[0] if single else shapes,
         scratch_shapes=list(scratch),
         **(specs or {}),
-        compiler_params=pltpu.CompilerParams(vmem_limit_bytes=16 << 20),
+        compiler_params=pltpu.CompilerParams(vmem_limit_bytes=40 << 20),
         cost_estimate=pl.CostEstimate(flops=flops, bytes_accessed=data, transcendentals=0),
     )
     return built
@@ -54,15 +54,9 @@
     return total
 
 
-def y_faces(krylov, low, high, done):
-    copies = [
-        pltpu.make_async_copy(krylov.at[:, :, y, :], out, done.at[k])
-        for k, (out, y) in enumerate(((low, 0), (high, 7)))
-    ]
-    for copy in copies:
-        copy.start()
-    for copy in copies:
-        copy.wait()
+def y_faces(krylov, low, high):
+    low[...] = krylov[:, :, 0, :]
+    high[...] = krylov[:, :, 7, :]
 
 
 def number(a, b, c):
@@ -238,7 +232,7 @@
         edge_y[side] = total
 
 
-def z_faces(odd, z_high, z_low, edge_y, x_low, x_high, near, far):
+def z_faces(z_high, z_low, edge_y, x_low, x_high, near, far):
     lane = lanes((8, 128))
     values = []
     for side, own in enumerate((z_high, z_low)):
@@ -251,7 +245,7 @@
                     part = roll(face[first : first + 8, :], place + 1 - side, 1)
                     value = jnp.where(lane == place, part, value)
             values.append(value)
-    flipped = odd[0] == 1
+    flipped = jnp.bitwise_and(lax.axis_index("gz"), 1) == 1
     for group in range(5):
         high, low = values[group], values[5 + group]
         near[group * 8 : group * 8 + 8, :] = jnp.where(flipped, low, high)
@@ -298,12 +292,12 @@
     partial[...] = fold_rows(product[0:128] + product[128:256])
 
 
-def finish(scale, odd, near, far, face_z, edge_basis, partial, gram, columns, payload):
+def finish(scale, near, far, face_z, edge_basis, partial, gram, columns, payload):
     row = rows((8, 128))
     lane = lanes((8, 128))
     for j in range(16):
         columns[j * 8 : j * 8 + 8, :] = jnp.zeros((8, 128), F32)
-    flipped = odd[0] == 1
+    flipped = jnp.bitwise_and(lax.axis_index("gz"), 1) == 1
     for side in range(2):
         pair = (far, near) if side == 0 else (near, far)
         received = jnp.where(flipped, pair[1][...], pair[0][...])
@@ -394,14 +388,7 @@
     cells = krylov[0].size * lax.axis_size("gx") * lax.axis_size("gy") * lax.axis_size("gz")
     scale = 1.0 / cells
     face = like((16, 16, 128))
-    low, high = call(
-        "y_faces",
-        y_faces,
-        (face, face),
-        scratch=[pltpu.SemaphoreType.DMA((2,))],
-        data=1 << 18,
-        specs={"in_specs": [pl.BlockSpec(memory_space=pltpu.HBM)]},
-    )(pltpu.with_memory_space_constraint(krylov, pltpu.HBM))
+    low, high = call("y_faces", y_faces, (face, face), data=1 << 20)(krylov)
     y_low, y_high = shifted(low, high, "gy")
     small = like((4, 8, 128))
     image, z_high, z_low, face_x, face_y, face_z = call(
@@ -435,12 +422,9 @@
         data=2 << 20,
     )(basis, y_low, y_high)
     end = like((40, 128))
-    odd = jnp.bitwise_and(lax.axis_index("gz"), 1).astype(jnp.int32).reshape(1)
-    scalar = pl.BlockSpec(memory_space=pltpu.SMEM)
-    block = pl.BlockSpec()
-    near, far = call(
-        "z_faces", z_faces, (end, end), data=1 << 18, specs={"in_specs": [scalar] + [block] * 5}
-    )(odd, z_high, z_low, edge_y, x_low, x_high)
+    near, far = call("z_faces", z_faces, (end, end), data=1 << 18)(
+        z_high, z_low, edge_y, x_low, x_high
+    )
     count = lax.axis_size("gz")
     near = lax.ppermute(near, "gz", [(i, i ^ 1) for i in range(count)])
     inner = range(1, count - 1)
@@ -458,8 +442,7 @@
         lambda *refs: finish(scale, *refs),
         (like((128, 128)), like((16, 128))),
         data=1 << 18,
-        specs={"in_specs": [scalar] + [block] * 6},
-    )(odd, near, far, face_z, edge_basis, partial, gram)
+    )(near, far, face_z, edge_basis, partial, gram)
     payload = summed(payload, "gz")
     payload = summed(payload, "gx")
     parts = summed(payload, "gy", last=True)

time: 81.3 us -> 77 us (0.947)
  Pallas kernels: 14.3 us -> 10.9 us
  blocking collectives: 44.1 us -> 42.9 us
  waiting for transfers between devices: 4.59 us -> 5.79 us
    pallas_call x2, Pallas kernels: 2.13 us -> 0.28 us  [the longest x1 0.14 us: local(): call('z_faces', z_faces, (end, end), data=1 << 18)]
    all_to_all x3, blocking collectives: 44.1 us -> 42.9 us  [summed(): parts = lax.all_to_all(copies, axis, 0, 0)]
    pallas_call x1, Pallas kernels: 3.11 us -> 2.16 us  [local(): call('corrections', corrections, (like((16, 16, 8, 128)), like((16, 256))...]
    ppermute x2, waiting for transfers between devices: 4.58 us -> 5.41 us  [shifted(): lax.ppermute(low_out, axis, backward)]
    unnamed x20 -> x8, local copies, waits for them, and re-layouts: 1.95 us -> 1.23 us
  transfers between devices with their start and end apart: 6 -> 6, of which waited for: 1 -> 3; matrix products, arithmetic and copies ran while one was open for 0% -> 0% of each run, Pallas kernels for 11% -> 10%
where the time goes in v4:
time: 77 us; the launch traced here: 76.6 us
  blocking collectives  42.9 us (56%)
  starting transfers between devices  15 us (19%)
  Pallas kernels  10.9 us (14%)
  waiting for transfers between devices  5.79 us (8%)
  local copies, waits for them, and re-layouts  1.25 us (2%)
  between operations  0.8 us (1%)
    all_to_all x3, blocking collectives, summed(): parts = lax.all_to_all(copies, axis, 0, 0)  42.9 us
    ppermute x2, starting transfers between devices, shifted(): lax.ppermute(high_out, axis, forward)  7.9 us
    ppermute x2, waiting for transfers between devices, shifted(): lax.ppermute(low_out, axis, backward)  5.41 us
    pallas_call x1, Pallas kernels, local(): call('interior', interior, (like((16, 16, 8, 128)), small, small, like((2...  4.35 us
    ppermute x2, starting transfers between devices, shifted(): lax.ppermute(low_out, axis, backward)  2.58 us
    ppermute x1, starting transfers between devices, local(): far = lax.ppermute(far, 'gz', [(i, (i + 1 ^ 1) - 1) for i in inner])  2.55 us
    pallas_call x1, Pallas kernels, local(): call('project', project, (like((16, 16, 8, 128)), like((16, 32))), scratc...  2.34 us
    pallas_call x1, Pallas kernels, local(): call('corrections', corrections, (like((16, 16, 8, 128)), like((16, 256))...  2.16 us
  transfers between devices with their start and end apart: 6, of which 3 were waited for; matrix products, arithmetic and copies ran while one was open for 0% of the time, Pallas kernels for 10%

profile of v4, /device:TPU:2, one launch (start us, length us, event | category | flops | bytes accessed | tf_op | source)
XLA Modules:
  0.0 76.6 jit_solution(180729875012898768)
XLA Ops:
  0.6 0.0 copy-start
  0.6 1.2 %copy-done = f32[16,16,8,128]{3,2,1,0:T(8,128)S(1)} copy-done((f32[16,16,8,128]{3,2,1,0:T(8,128)S(1)}, f32[16,16,8,128]{3,2,1,0:T(8,128)}, u32[]{:S(2)}) %copy-start) | copy-done | bytes 1048600
  1.9 0.0 copy-start.2
  1.9 0.0 copy-start.3
  1.9 0.1 y_faces.1
  2.0 3.6 %collective-permute-start = (f32[16,16,128]{2,1,0:T(8,128)S(1)}, f32[16,16,128]{2,1,0:T(8,128)S(1)}, u32[]{:S(2)}, u32[]{:S(2)}) collective-permute-start(f32[16,16,128]{2,1,0:T(8,128)S(1)} %get-tuple-element.26), channel_id=1, source_target_pairs={{0,8},{8,16},{16,24},{24,32},{32,40},{40,48},{48,56},{1,9},{9,17},... | collective-permute-start | bytes 393224 | tf_op jit(solution)/shard_map/ppermute | solution.py:378
  5.6 1.3 %collective-permute-start.1 = (f32[16,16,128]{2,1,0:T(8,128)S(1)}, f32[16,16,128]{2,1,0:T(8,128)S(1)}, u32[]{:S(2)}, u32[]{:S(2)}) collective-permute-start(f32[16,16,128]{2,1,0:T(8,128)S(1)} %get-tuple-element.27), channel_id=1, source_target_pairs={{8,0},{16,8},{24,16},{32,24},{40,32},{48,40},{56,48},{9,1},{17,9},... | collective-permute-start | bytes 393224 | tf_op jit(solution)/shard_map/ppermute | solution.py:378
  6.9 0.0 copy-done.2
  6.9 0.0 copy-done.3
  7.0 4.4 %interior.1 = (f32[16,16,8,128]{3,2,1,0:T(8,128)S(1)}, f32[4,8,128]{2,1,0:T(8,128)S(1)}, f32[4,8,128]{2,1,0:T(8,128)S(1)}, f32[2,9,8,128]{3,2,1,0:T(8,128)S(1)},...) custom-call(f32[16,16,8,128]{3,2,1,0:T(8,128)S(1)} %copy-done, bf16[16,8,128]{2,1,0:T(8,128)(2,1)S(1)} %copy-done.3, ...), custom_call_target="tpu_custom_call" | custom-call | flops 16777216 | bytes 4194304 | tf_op jit(solution)/shard_map/interior/pallas_call | solution.py:394
  11.3 0.0 copy-start.1
  11.3 0.0 collective-permute-done.refs_1_.y_low
  11.3 1.2 %collective-permute-done.1.refs_2_.y_high = f32[16,16,128]{2,1,0:T(8,128)S(1)} collective-permute-done((f32[16,16,128]{2,1,0:T(8,128)S(1)}, f32[16,16,128]{2,1,0:T(8,128)S(1)}, u32[]{:S(2)}, u32[]{:S(2)}) %collective-permute-start.1) | collective-permute-done | bytes 131104 | tf_op jit(solution)/shard_map/ppermute | solution.py:378
  12.5 4.3 %collective-permute-start.2 = (f32[160,128]{1,0:T(8,128)S(1)}, f32[160,128]{1,0:T(8,128)S(1)}, u32[]{:S(2)}, u32[]{:S(2)}) collective-permute-start(f32[160,128]{1,0:T(8,128)S(1)} %get-tuple-element.29), channel_id=1, source_target_pairs={{0,64},{64,128},{128,192},{192,256},{256,320},{320,384},{384,448},... | collective-permute-start | bytes 245768 | tf_op jit(solution)/shard_map/ppermute | solution.py:378
  16.8 1.3 %collective-permute-start.3 = (f32[160,128]{1,0:T(8,128)S(1)}, f32[160,128]{1,0:T(8,128)S(1)}, u32[]{:S(2)}, u32[]{:S(2)}) collective-permute-start(f32[160,128]{1,0:T(8,128)S(1)} %get-tuple-element.30), channel_id=1, source_target_pairs={{64,0},{128,64},{192,128},{256,192},{320,256},{384,320},{448,384},... | collective-permute-start | bytes 245768 | tf_op jit(solution)/shard_map/ppermute | solution.py:378
  18.1 0.0 copy-done.1
  18.1 1.1 %basis.1 = (bf16[256,2048]{1,0:T(8,128)(2,1)S(1)}, f32[8,128]{1,0:T(8,128)S(1)}, bf16[256,128]{1,0:T(8,128)(2,1)S(1)}, f32[2,8,128]{2,1,0:T(8,128)S(1)}) custom-call(bf16[32,16,8,128]{3,2,1,0:T(8,128)(2,1)S(1)} %copy-done.1, f32[16,16,128]{2,1,0:T(8,128)S(1)} %collective-permute-done.refs_1_.y_low, f32[16,16,128]{2,1,0:T(8,128)S(1)} %collective-permute-done.1.refs_2_.y_high), custom_call_target="tpu_custom_call" | custom-call | flops 268435456 | bytes 2097152 | tf_op jit(solution)/shard_map/basis/pallas_call | solution.py:412
  19.3 0.0 collective-permute-done.2.x_low
  19.3 4.2 %collective-permute-done.3.x_high = f32[160,128]{1,0:T(8,128)S(1)} collective-permute-done((f32[160,128]{1,0:T(8,128)S(1)}, f32[160,128]{1,0:T(8,128)S(1)}, u32[]{:S(2)}, u32[]{:S(2)}) %collective-permute-start.3) | collective-permute-done | bytes 81952 | tf_op jit(solution)/shard_map/ppermute | solution.py:378
  23.5 0.1 z_faces.1
  23.7 1.9 %collective-permute-start.4 = (f32[40,128]{1,0:T(8,128)S(1)}, f32[40,128]{1,0:T(8,128)S(1)}, u32[]{:S(2)}, u32[]{:S(2)}) collective-permute-start(f32[40,128]{1,0:T(8,128)S(1)} %get-tuple-element.31), channel_id=1, source_target_pairs={{0,1},{1,0},{2,3},{3,2},{4,5},{5,4},{6,7},{7,6},{8,9},{9,8},{10,11... | collective-permute-start | bytes 61448 | tf_op jit(solution)/shard_map/ppermute | solution.py:429
  25.6 2.5 %collective-permute-start.5 = (f32[40,128]{1,0:T(8,128)S(1)}, f32[40,128]{1,0:T(8,128)S(1)}, u32[]{:S(2)}, u32[]{:S(2)}) collective-permute-start(f32[40,128]{1,0:T(8,128)S(1)} %get-tuple-element.32), channel_id=1, source_target_pairs={{1,2},{2,1},{3,4},{4,3},{5,6},{6,5},{9,10},{10,9},{11,12},{12,11},... | collective-permute-start | bytes 61448 | tf_op jit(solution)/shard_map/ppermute | solution.py:431
  28.1 2.2 %corrections.1 = (f32[16,16,8,128]{3,2,1,0:T(8,128)S(1)}, f32[16,256]{1,0:T(8,128)S(1)}) custom-call(f32[16,16,128]{2,1,0:T(8,128)S(1)} %collective-permute-done.refs_1_.y_low, f32[16,16,128]{2,1,0:T(8,128)S(1)} %collective-permute-done.1.refs_2_.y_high, f32[160,128]{1,0:T(8,128)S(1)} %collective-permute-done.2.x_low, ...), custom_call_target="tpu_custom_call" | custom-call | flops 268435456 | bytes 4194304 | tf_op jit(solution)/shard_map/corrections/pallas_call | solution.py:432
  30.3 0.0 collective-permute-done.4.refs_0_
  30.3 0.4 collective-permute-done.5.refs_1_
  30.7 0.6 finish.1
  31.3 8.9 %all_to_all.15 = f32[8,16,128]{2,1,0:T(8,128)S(1)} all-to-all(f32[8,16,128]{2,1,0:T(8,128)S(1)} %broadcast_in_dim.6), channel_id=1, replica_groups=mesh['gx'=8,'gy'=8,'gz'=8] {'gz'}, dimensions={0} | all-to-all | bytes 131072 | tf_op jit(solution)/shard_map/all_to_all | solution.py:383
  40.2 17.5 %all_to_all.16 = f32[8,16,128]{2,1,0:T(8,128)S(1)} all-to-all(f32[8,16,128]{2,1,0:T(8,128)S(1)} %broadcast_in_dim.7), channel_id=1, replica_groups=mesh['gx'=8,'gy'=8,'gz'=8] {'gx'}, dimensions={0} | all-to-all | bytes 131072 | tf_op jit(solution)/shard_map/all_to_all | solution.py:383
  57.8 16.5 %all_to_all.17.parts = f32[8,16,128]{2,1,0:T(8,128)S(1)} all-to-all(f32[8,16,128]{2,1,0:T(8,128)S(1)} %broadcast_in_dim.8), channel_id=1, replica_groups=mesh['gx'=8,'gy'=8,'gz'=8] {'gy'}, dimensions={0} | all-to-all | bytes 131072 | tf_op jit(solution)/shard_map/all_to_all | solution.py:383
  74.3 2.3 %project.1 = (f32[16,16,8,128]{3,2,1,0:T(8,128)}, f32[16,32]{1,0:T(8,128)}) custom-call(f32[8,16,128]{2,1,0:T(8,128)S(1)} %all_to_all.17.parts, f32[16,16,8,128]{3,2,1,0:T(8,128)S(1)} %get-tuple-element.42.given, f32[128,128]{1,0:T(8,128)S(1)} %get-tuple-element.43.columns, bf16[256,2048]{1,0:T(8,128)(2,1)S(1)} %get-tuple-element.37.flat), custom_call_target="tpu_custom_call" | custom-call | flops 268435456 | bytes 3145728 | tf_op jit(solution)/shard_map/project/pallas_call | solution.py:449
  (6 shorter events, 0.1 us)
Async XLA Ops:
  0.6 1.2 %copy-start = (f32[16,16,8,128]{3,2,1,0:T(8,128)S(1)}, f32[16,16,8,128]{3,2,1,0:T(8,128)}, u32[]{:S(2)}) copy-start(f32[16,16,8,128]{3,2,1,0:T(8,128)} %krylov.5) | copy-start | bytes 3145732
  1.9 5.1 %copy-start.2 = (bf16[26,16,8,128]{3,2,1,0:T(8,128)(2,1)S(1)}, bf16[26,16,8,128]{3,2,1,0:T(8,128)(2,1)}, u32[]{:S(2)}) copy-start(bf16[26,16,8,128]{3,2,1,0:T(8,128)(2,1)} %couplings.1) | copy-start | bytes 2555908
  1.9 5.1 %copy-start.3 = (bf16[16,8,128]{2,1,0:T(8,128)(2,1)S(1)}, bf16[16,8,128]{2,1,0:T(8,128)(2,1)}, u32[]{:S(2)}) copy-start(bf16[16,8,128]{2,1,0:T(8,128)(2,1)} %center.1) | copy-start | bytes 98308
  2.0 9.3 %collective-permute-start = (f32[16,16,128]{2,1,0:T(8,128)S(1)}, f32[16,16,128]{2,1,0:T(8,128)S(1)}, u32[]{:S(2)}, u32[]{:S(2)}) collective-permute-start(f32[16,16,128]{2,1,0:T(8,128)S(1)} %get-tuple-element.26), channel_id=1, source_target_pairs={{0,8},{8,16},{16,24},{24,32},{32,40},{40,48},{48,56},{1,9},{9,17},... | collective-permute-start | bytes 393224 | tf_op jit(solution)/shard_map/ppermute | solution.py:378
  5.6 6.9 %collective-permute-start.1 = (f32[16,16,128]{2,1,0:T(8,128)S(1)}, f32[16,16,128]{2,1,0:T(8,128)S(1)}, u32[]{:S(2)}, u32[]{:S(2)}) collective-permute-start(f32[16,16,128]{2,1,0:T(8,128)S(1)} %get-tuple-element.27), channel_id=1, source_target_pairs={{8,0},{16,8},{24,16},{32,24},{40,32},{48,40},{56,48},{9,1},{17,9},... | collective-permute-start | bytes 393224 | tf_op jit(solution)/shard_map/ppermute | solution.py:378
  11.3 6.8 %copy-start.1 = (bf16[32,16,8,128]{3,2,1,0:T(8,128)(2,1)S(1)}, bf16[32,16,8,128]{3,2,1,0:T(8,128)(2,1)}, u32[]{:S(2)}) copy-start(bf16[32,16,8,128]{3,2,1,0:T(8,128)(2,1)} %refs_0_.1) | copy-start | bytes 3145732
  12.5 6.7 %collective-permute-start.2 = (f32[160,128]{1,0:T(8,128)S(1)}, f32[160,128]{1,0:T(8,128)S(1)}, u32[]{:S(2)}, u32[]{:S(2)}) collective-permute-start(f32[160,128]{1,0:T(8,128)S(1)} %get-tuple-element.29), channel_id=1, source_target_pairs={{0,64},{64,128},{128,192},{192,256},{256,320},{320,384},{384,448},... | collective-permute-start | bytes 245768 | tf_op jit(solution)/shard_map/ppermute | solution.py:378
  16.8 6.7 %collective-permute-start.3 = (f32[160,128]{1,0:T(8,128)S(1)}, f32[160,128]{1,0:T(8,128)S(1)}, u32[]{:S(2)}, u32[]{:S(2)}) collective-permute-start(f32[160,128]{1,0:T(8,128)S(1)} %get-tuple-element.30), channel_id=1, source_target_pairs={{64,0},{128,64},{192,128},{256,192},{320,256},{384,320},{448,384},... | collective-permute-start | bytes 245768 | tf_op jit(solution)/shard_map/ppermute | solution.py:378
  23.7 6.7 %collective-permute-start.4 = (f32[40,128]{1,0:T(8,128)S(1)}, f32[40,128]{1,0:T(8,128)S(1)}, u32[]{:S(2)}, u32[]{:S(2)}) collective-permute-start(f32[40,128]{1,0:T(8,128)S(1)} %get-tuple-element.31), channel_id=1, source_target_pairs={{0,1},{1,0},{2,3},{3,2},{4,5},{5,4},{6,7},{7,6},{8,9},{9,8},{10,11... | collective-permute-start | bytes 61448 | tf_op jit(solution)/shard_map/ppermute | solution.py:429
  25.6 5.1 %collective-permute-start.5 = (f32[40,128]{1,0:T(8,128)S(1)}, f32[40,128]{1,0:T(8,128)S(1)}, u32[]{:S(2)}, u32[]{:S(2)}) collective-permute-start(f32[40,128]{1,0:T(8,128)S(1)} %get-tuple-element.32), channel_id=1, source_target_pairs={{1,2},{2,1},{3,4},{4,3},{5,6},{6,5},{9,10},{10,9},{11,12},{12,11},... | collective-permute-start | bytes 61448 | tf_op jit(solution)/shard_map/ppermute | solution.py:431
